TPU v7x, 512 devices: a whole 4x8x8 slice. The times are simulated.
512 devices in a mesh: dp: 64 (over x, y, core), mp: 8 (over z).
Axes of the slice: x: 4, y: 8, z: 8, core: 2. Of those that a mesh axis runs over, the one named last changes fastest.
Arguments:
- hidden: bfloat16 [98304, 3584], P('dp', 'mp'), may hold values from -6 to 6
- frozen_value_weight: bfloat16 [3584, 512], P('mp'), may hold values from -0.09375 to 0.09375
- adapter_down_weight: bfloat16 [64, 3584, 32], P('dp', 'mp'), may hold values from -0.09375 to 0.09375
- adapter_up_weight: bfloat16 [64, 32, 512], P('dp', None, 'mp'), may hold values from -1 to 1
- value_output_gradient: bfloat16 [98304, 512], P('dp', 'mp'), may hold values from -6 to 6
- sequence_tenant_index: int32 [128], P('dp'), may hold values from 0 to 63
- tenant_slot_table: int32 [64], replicated, may hold values from 0 to 63, each once
Outputs:
- values: bfloat16 [98304, 512], P('dp', 'mp')
- hidden_grad: bfloat16 [98304, 3584], P('dp', 'mp')
- down_grad: float32 [64, 3584, 32], P('dp', 'mp')
- up_grad: float32 [64, 32, 512], P('dp', None, 'mp')
Inputs may be any that keep to these rules, and one draw needn't show every extreme that they name: `sequence_tenant_index`: tenant of each sequence; several sequences may share a tenant. `tenant_slot_table`: every slot holds exactly one tenant.
All inputs are finite; a program needn't handle non-finite values.
Results may differ from a plain program's by a relative error of at most 0.0039.
Values may be sent and summed in bfloat16 or wider, within the bound.
A program may use at most 128 MiB of HBM per device.

v0:
```python
import jax
import jax.numpy as jnp
from jax import lax
from jax.sharding import PartitionSpec as P

highest_precision = lax.Precision.HIGHEST


def from_everyone(shard, axis):
    copies = jnp.broadcast_to(shard, (lax.axis_size(axis), *shard.shape))
    return lax.all_to_all(copies, axis, split_axis=0, concat_axis=0, tiled=True)


def taken_together(shard, axis):
    everything = from_everyone(shard, axis)
    return jnp.sum(everything, axis=0)


def sent_together(arrays, axis, split_dim, concat_dim, along):
    columns = [a.reshape(*a.shape[:along], -1) for a in arrays]
    both = jnp.concatenate(columns, axis=along)
    whole, at, gathered = (
        lax.all_to_all(both, axis, split_axis=split_dim, concat_axis=concat_dim, tiled=True),
        0,
        [],
    )
    for a, column in zip(arrays, columns):
        section = whole[..., at : at + column.shape[along]]
        gathered.append(section.reshape(*section.shape[:along], *a.shape[along:]))
        at += column.shape[along]
    return tuple(gathered)


def local(
    hidden,
    frozen_value_weight,
    adapter_down_weight,
    adapter_up_weight,
    value_output_gradient,
    sequence_tenant_index,
    tenant_slot_table,
):
    seq_count = sequence_tenant_index.shape[0]
    token_rows, shard_width = hidden.shape
    reduced_rank_hidden = adapter_down_weight.shape[2]
    column_total = value_output_gradient.shape[1]
    seq_len = token_rows // seq_count
    down_all, up_all = (
        lax.all_gather(adapter_down_weight, "dp", axis=0, tiled=True),
        lax.all_gather(adapter_up_weight, "dp", axis=0, tiled=True),
    )
    slot_count = down_all.shape[0]
    slot_ids = tenant_slot_table[sequence_tenant_index]
    pick_rows = slot_ids[:, None] == jnp.arange(slot_count, dtype=jnp.int32)[None, :]
    pick_half = pick_rows.astype(jnp.bfloat16)
    pick_full = pick_rows.astype(jnp.float32)
    chosen_down_factor = jnp.einsum(
        "st,tdr->sdr", pick_half, down_all, preferred_element_type=jnp.float32
    ).astype(jnp.bfloat16)
    sequence_input_rows = hidden.reshape(seq_count, seq_len, shard_width)
    seq_grads = value_output_gradient.reshape(seq_count, seq_len, column_total)
    seq_grads_full = seq_grads.astype(jnp.float32)
    reduced_rank_partial = jnp.einsum(
        "bcp,bpk->bck", sequence_input_rows, chosen_down_factor, preferred_element_type=jnp.float32
    )
    frozen_value_output = jnp.dot(hidden, frozen_value_weight, preferred_element_type=jnp.float32)
    chosen_up_factor = jnp.einsum(
        "st,trk->srk", pick_full, up_all.astype(jnp.float32), precision=highest_precision
    )
    reduced_total = lax.psum_scatter(frozen_value_output, "mp", scatter_dimension=1, tiled=True)
    reduced_rank_full = taken_together(reduced_rank_partial, "mp")
    adapter_shard_output = jnp.einsum(
        "pmy,pyd->pmd", reduced_rank_full, chosen_up_factor, precision=highest_precision
    )
    reduced_total = reduced_total + adapter_shard_output.reshape(token_rows, column_total)
    values = reduced_total.astype(jnp.bfloat16)
    back_part = jnp.einsum(
        "slk,srk->slr", seq_grads_full, chosen_up_factor, precision=highest_precision
    )
    back_full = taken_together(back_part, "mp")
    up_seq = jnp.einsum(
        "slr,slk->srk", reduced_rank_full, seq_grads_full, precision=highest_precision
    )
    backward_lowrank_term = back_full.astype(jnp.bfloat16)
    adapter_gradient = jnp.einsum(
        "abq,ajq->abj",
        backward_lowrank_term,
        chosen_down_factor,
        preferred_element_type=jnp.float32,
    )
    hidden_grad = (
        lax.dot_general(
            lax.all_gather(value_output_gradient, "mp", axis=1, tiled=True),
            frozen_value_weight,
            (((1,), (1,)), ((), ())),
            preferred_element_type=jnp.float32,
        )
        + adapter_gradient.reshape(token_rows, shard_width)
    ).astype(jnp.bfloat16)
    sequence_down_factor = jnp.einsum(
        "ikp,ikf->ipf",
        sequence_input_rows,
        backward_lowrank_term,
        preferred_element_type=jnp.float32,
    )
    down_slots = jnp.einsum(
        "st,sdr->tdr", pick_full, sequence_down_factor, precision=highest_precision
    )
    up_slots = jnp.einsum("st,srk->trk", pick_full, up_seq, precision=highest_precision)
    down_home, up_home = sent_together((down_slots, up_slots), "dp", 0, 0, 1)
    owners = lax.axis_size("dp")
    down_grad = down_home.reshape(owners, -1, shard_width, reduced_rank_hidden).sum(axis=0)
    up_grad = up_home.reshape(owners, -1, reduced_rank_hidden, column_total).sum(axis=0)
    return (values, hidden_grad, down_grad, up_grad)


def solution(mesh):
    return jax.shard_map(
        local,
        mesh=mesh,
        in_specs=(
            P("dp", "mp"),
            P("mp", None),
            P("dp", "mp", None),
            P("dp", None, "mp"),
            P("dp", "mp"),
            P("dp"),
            P(),
        ),
        out_specs=(P("dp", "mp"), P("dp", "mp"), P("dp", "mp", None), P("dp", None, "mp")),
        check_vma=False,
    )
```

profile of v0, /device:TPU:1, one launch (start us, length us, event | category | flops | bytes accessed | tf_op | source)
XLA Modules:
  0.0 311.0 jit_solution(10692167408571343461)
XLA Ops:
  8.0 0.0 copy-start
  8.0 0.0 all-gather.3.cloned.1.call-start
  8.1 0.7 all-gather.3.cloned.1.call-update
  8.7 0.7 compare_select_fusion
  9.4 1.3 gather_fusion
  10.7 54.5 %all_gather.10 = bf16[64,32,64]{2,1,0:T(8,128)(2,1)S(1)} all-gather(bf16[1,32,64]{2,1,0:T(8,128)(2,1)} %param.10), channel_id=1, replica_groups=mesh['dp'=64,'mp'=8] {'dp'}, dimensions={0}, use_global_device_ids=true | all-gather | bytes 266240 | tf_op jit(solution)/shard_map/all_gather | solution.py:50
  65.2 0.3 fusion.18
  65.4 1.1 convolution_bitcast_fusion.2
  66.6 1.3 broadcast_in_dim.13
  67.9 8.5 %all-to-all-start.1 = ((f32[8,2,768,32]{2,3,1,0:T(8,128)}), f32[8,2,768,32]{2,3,1,0:T(8,128)S(1)}, u32[]{:S(2)}, u32[]{:S(2)}) async-start(f32[8,2,768,32]{2,3,1,0:T(8,128)} %broadcast_in_dim.13), calls=%async_computation.2 | async-start | bytes 3145728 | tf_op jit(solution)/shard_map/all_to_all | solution.py:11
  76.4 24.3 %all-gather.3.cloned.1.call-done = bf16[64,448,32]{1,2,0:T(8,128)(2,1)} async-done(((bf16[1,448,32]{1,2,0:T(8,128)(2,1)}), bf16[64,448,32]{1,2,0:T(8,128)(2,1)}) %all-gather.3.cloned.1.call-update) | async-done | bytes 1835024 | tf_op jit(solution)/shard_map/all_gather | solution.py:49
  100.7 3.9 %fusion.15 = bf16[2,448,32]{1,0,2:T(2,128)(2,1)S(1)} fusion(bf16[64,448,32]{1,2,0:T(8,128)(2,1)} %all-gather.3.cloned.1.call-done, s32[2]{0:T(128)S(1)} %gather_fusion), kind=kOutput, calls=%fused_computation.19 | convolution fusion | flops 3698816 | bytes 1892360 | tf_op jit(solution)/shard_map/st,tdr->sdr/dot_general | solution.py:57
  104.6 0.6 copy-done.5
  105.3 1.0 fusion.9
  106.3 10.5 %all-to-all-done.1 = f32[8,2,768,32]{2,3,1,0:T(8,128)S(1)} async-done(((f32[8,2,768,32]{2,3,1,0:T(8,128)}), f32[8,2,768,32]{2,3,1,0:T(8,128)S(1)}, u32[]{:S(2)}, u32[]{:S(2)}) %all-to-all-start.1) | async-done | bytes 1572896 | tf_op jit(solution)/shard_map/all_to_all | solution.py:11
  116.8 2.2 broadcast_in_dim.12
  119.1 4.3 %all-to-all-start = ((f32[8,2,768,32]{2,3,1,0:T(8,128)}), f32[8,2,768,32]{2,3,1,0:T(8,128)}, u32[]{:S(2)}, u32[]{:S(2)}) async-start(f32[8,2,768,32]{2,3,1,0:T(8,128)} %broadcast_in_dim.12), calls=%async_computation.1 | async-start | bytes 3145728 | tf_op jit(solution)/shard_map/all_to_all | solution.py:11
  123.4 0.0 all-gather.5.cloned.1.call-start
  123.4 0.5 all-gather.5.cloned.1.call-update
  123.9 0.1 reduce_sum.41
  124.0 0.5 fusion.12
  124.5 3.9 %fusion.25 = f32[64,448,32]{1,0,2:T(8,128)} fusion(f32[2,448,32]{1,2,0:T(8,128)S(1)} %fusion.12, s32[2]{0:T(128)S(1)} %gather_fusion), kind=kOutput, calls=%fused_computation.29 | convolution fusion | flops 22020224 | bytes 3784712 | tf_op jit(solution)/shard_map/st,sdr->tdr/dot_general | solution.py:106
  128.4 6.7 %copy.51 = f32[64,448,32]{0,2,1:T(8,128)} copy(f32[64,448,32]{1,0,2:T(8,128)} %fusion.25) | data formatting | bytes 7340032 | tf_op jit(solution)/shard_map/st,sdr->tdr/dot_general | solution.py:106
  135.0 37.6 %all-to-all-done = f32[8,2,768,32]{2,3,1,0:T(8,128)} async-done(((f32[8,2,768,32]{2,3,1,0:T(8,128)}), f32[8,2,768,32]{2,3,1,0:T(8,128)}, u32[]{:S(2)}, u32[]{:S(2)}) %all-to-all-start) | async-done | bytes 1572896 | tf_op jit(solution)/shard_map/all_to_all | solution.py:11
  172.6 1.5 reduce_sum.40
  174.1 0.0 copy-start.3
  174.1 0.3 fusion.20
  174.4 1.1 fusion.31
  175.5 7.0 %maximum_bitcast_fusion = f32[64,1,16384]{0,2,1:T(8,128)} fusion(f32[64,2048]{0,1:T(8,128)S(1)} %bitcast.58, f32[64,14336]{0,1:T(8,128)} %bitcast.52), kind=kLoop, calls=%fused_computation.1 | loop fusion | flops 1048576 | bytes 8388608 | tf_op jit(solution)/shard_map/all_to_all | solution.py:23
  182.5 11.9 %copy.56 = f32[64,1,16384]{2,1,0:T(1,128)} copy(f32[64,1,16384]{0,2,1:T(8,128)} %maximum_bitcast_fusion) | data formatting | bytes 8388608 | tf_op jit(solution)/shard_map/all_to_all | solution.py:23
  194.4 6.9 %all-to-all-start.2 = ((f32[64,1,16384]{2,1,0:T(1,128)}), f32[64,1,16384]{2,1,0:T(1,128)}, u32[]{:S(2)}, u32[]{:S(2)}) async-start(f32[64,1,16384]{2,1,0:T(1,128)} %copy.56), calls=%async_computation.3 | async-start | bytes 8388608 | tf_op jit(solution)/shard_map/all_to_all | solution.py:23
  201.3 0.0 reduce-scatter.2.cloned.1.call-start
  201.3 2.7 fusion.43
  204.0 0.0 reduce-scatter.2.cloned.1.call-update
  204.0 0.8 copy-done.6
  204.9 0.6 convolution_bitcast_fusion
  205.4 0.4 copy.64
  205.8 0.0 all-gather.5.cloned.1.call-done
  205.9 3.4 %fusion = bf16[1536,448]{0,1:T(8,128)(2,1)} fusion(f32[1536,448]{0,1:T(8,128)S(1)} %bitcast.57, bf16[448,512]{1,0:T(8,128)(2,1)S(1)} %copy-done, bf16[1536,512]{0,1:T(8,128)(2,1)} %all-gather.5.cloned.1.call-done), kind=kOutput, calls=%fused_computation.5 | convolution fusion | flops 706019328 | bytes 6160384 | tf_op jit(solution)/shard_map/dot_general | solution.py:92
  209.3 0.5 convolution_bitcast_fusion.1
  209.8 40.3 %reduce-scatter.2.cloned.1.call-done = f32[1536,64]{0,1:T(8,128)} async-done(((f32[1536,512]{0,1:T(8,128)}), f32[1536,64]{0,1:T(8,128)}) %reduce-scatter.2.cloned.1.call-update) | async-done | bytes 393232 | tf_op jit(solution)/shard_map/reduce_scatter | solution.py:70
  250.1 1.7 add_convert_fusion
  251.8 45.3 %all-to-all-done.2 = f32[64,1,16384]{2,1,0:T(1,128)} async-done(((f32[64,1,16384]{2,1,0:T(1,128)}), f32[64,1,16384]{2,1,0:T(1,128)}, u32[]{:S(2)}, u32[]{:S(2)}) %all-to-all-start.2) | async-done | bytes 4194336 | tf_op jit(solution)/shard_map/all_to_all | solution.py:23
  297.1 4.6 %copy.104 = f32[64,1,16384]{2,0,1:T(8,128)S(1)} copy(f32[64,1,16384]{2,1,0:T(1,128)} %all-to-all-done.2) | data formatting | bytes 8388608
  301.7 0.3 slice_reduce_fusion
  302.0 0.1 reduce_sum.43
  302.1 0.7 copy.57
  302.8 0.7 reduce_sum.45
  (13 shorter events, 0.1 us)
Async XLA Ops:
  8.0 193.3 %copy-start = (bf16[448,512]{1,0:T(8,128)(2,1)S(1)}, bf16[448,512]{1,0:T(8,128)(2,1)}, u32[]{:S(2)}) copy-start(bf16[448,512]{1,0:T(8,128)(2,1)} %param.8) | copy-start | bytes 1376260
  8.0 92.7 %all-gather.3.cloned.1.call-start = ((), (), s32[]{:S(2)}) async-start(), calls=%async_computation.5 | async-start | bytes 2129920 | tf_op jit(solution)/shard_map/all_gather | solution.py:49
  67.9 37.3 %copy-start.1 = (bf16[1536,448]{0,1:T(8,128)(2,1)S(1)}, bf16[1536,448]{0,1:T(8,128)(2,1)}, u32[]{:S(2)}) copy-start(bf16[1536,448]{0,1:T(8,128)(2,1)} %param.7) | copy-start | bytes 4128772
  67.9 48.9 %all-to-all-start.1 = ((f32[8,2,768,32]{2,3,1,0:T(8,128)}), f32[8,2,768,32]{2,3,1,0:T(8,128)S(1)}, u32[]{:S(2)}, u32[]{:S(2)}) async-start(f32[8,2,768,32]{2,3,1,0:T(8,128)} %broadcast_in_dim.13), calls=%async_computation.2 | async-start | bytes 3145728 | tf_op jit(solution)/shard_map/all_to_all | solution.py:11
  104.6 0.6 copy-start.5
  119.1 53.5 %all-to-all-start = ((f32[8,2,768,32]{2,3,1,0:T(8,128)}), f32[8,2,768,32]{2,3,1,0:T(8,128)}, u32[]{:S(2)}, u32[]{:S(2)}) async-start(f32[8,2,768,32]{2,3,1,0:T(8,128)} %broadcast_in_dim.12), calls=%async_computation.1 | async-start | bytes 3145728 | tf_op jit(solution)/shard_map/all_to_all | solution.py:11
  123.4 82.5 %all-gather.5.cloned.1.call-start = ((), (), s32[]{:S(2)}) async-start(), calls=%async_computation.6 | async-start | bytes 1769472 | tf_op jit(solution)/shard_map/all_gather | solution.py:93
  128.4 45.7 %copy-start.2 = (bf16[1536,64]{0,1:T(8,128)(2,1)S(1)}, bf16[1536,64]{0,1:T(8,128)(2,1)}, u32[]{:S(2)}) copy-start(bf16[1536,64]{0,1:T(8,128)(2,1)} %param.11) | copy-start | bytes 589828
  174.1 8.4 %copy-start.3 = (f32[2,768,32]{1,2,0:T(8,128)}, f32[2,768,32]{1,2,0:T(8,128)S(1)}, u32[]{:S(2)}) copy-start(f32[2,768,32]{1,2,0:T(8,128)S(1)} %reduce_sum.40) | copy-start | bytes 589828
  194.4 102.8 %all-to-all-start.2 = ((f32[64,1,16384]{2,1,0:T(1,128)}), f32[64,1,16384]{2,1,0:T(1,128)}, u32[]{:S(2)}, u32[]{:S(2)}) async-start(f32[64,1,16384]{2,1,0:T(1,128)} %copy.56), calls=%async_computation.3 | async-start | bytes 8388608 | tf_op jit(solution)/shard_map/all_to_all | solution.py:23
  201.3 48.8 %reduce-scatter.2.cloned.1.call-start = ((), (), s32[]{:S(2)}) async-start(), calls=%async_computation.4 | async-start | bytes 3538944 | tf_op jit(solution)/shard_map/reduce_scatter | solution.py:70
  204.0 0.8 copy-start.6
  205.8 3.4 %copy-start.4 = (f32[2,768,32]{1,2,0:T(8,128)S(1)}, f32[2,768,32]{1,2,0:T(8,128)}, u32[]{:S(2)}) copy-start(f32[2,768,32]{1,2,0:T(8,128)} %copy-done.3) | copy-start | bytes 589828
Sparse Core Ops, SparseCore 0:
  12.2 88.4 all-gather.2
Sparse Core Ops, SparseCore 1:
  125.9 52.9 all-gather.4
  204.6 45.4 reduce-scatter.1
where the time goes:
time: 312 us; the launch traced here: 311 us
  waiting for transfers between devices  159 us (51%)
  blocking collectives  54.5 us (17%)
  local copies, waits for them, and re-layouts  31.3 us (10%)
  starting transfers between devices  19.8 us (6%)
  matrix products  19.2 us (6%)
  between operations  15.6 us (5%)
  other arithmetic  11.3 us (4%)
    all_gather x1, blocking collectives, local(): lax.all_gather(adapter_up_weight, 'dp', axis=0, tiled=True)  54.5 us
    all_to_all x2, waiting for transfers between devices, from_everyone(): return lax.all_to_all(copies, axis, split_axis=0, concat_axis=0, tiled=True)  48.1 us
    all_to_all x1, waiting for transfers between devices, sent_together(): lax.all_to_all(both, axis, split_axis=split_dim, concat_axis=concat_dim,...  45.3 us
    reduce_scatter x1, waiting for transfers between devices, local(): lax.psum_scatter(frozen_value_output, 'mp', scatter_dimension=1, tiled=True)  40.3 us
    all_gather x1, waiting for transfers between devices, local(): lax.all_gather(adapter_down_weight, 'dp', axis=0, tiled=True)  24.3 us
    all_to_all x2, starting transfers between devices, from_everyone(): return lax.all_to_all(copies, axis, split_axis=0, concat_axis=0, tiled=True)  12.8 us
    all_to_all x1, local copies, waits for them, and re-layouts, sent_together(): lax.all_to_all(both, axis, split_axis=split_dim, concat_axis=concat_dim,...  11.9 us
    all_to_all x1, other arithmetic, sent_together(): lax.all_to_all(both, axis, split_axis=split_dim, concat_axis=concat_dim,...  7.04 us
  transfers between devices with their start and end apart: 6, of which 5 were waited for; matrix products, arithmetic and copies ran while one was open for 17% of the time, Pallas kernels for 0%

commit v1 on v0

v1 whole, which is shorter than its diff:
```python
import functools

import jax
import jax.numpy as jnp
from jax import lax
from jax.experimental import pallas as pl
from jax.experimental.pallas import tpu as pltpu
from jax.sharding import PartitionSpec as P

F32 = jnp.float32
BF16 = jnp.bfloat16
MESH = pl.DeviceIdType.MESH
NY = 8


def nt(a, b):
    return lax.dot_general(a, b, (((1,), (1,)), ((), ())), preferred_element_type=F32)


def nn(a, b):
    return jnp.dot(a, b, preferred_element_type=F32)


def iota(shape, dim):
    return lax.broadcasted_iota(jnp.int32, shape, dim)


def onehot(mask):
    return jnp.where(mask, 1.0, 0.0).astype(BF16)


def split(v):
    hi = v.astype(BF16)
    return hi, (v - hi.astype(F32)).astype(BF16)


def kernel(
    ny, nl, nz,
    idx_ref, tab_ref, g_hbm, b_hbm, a_hbm, w_hbm, x_hbm,
    values_ref, hgrad_hbm, down_ref, up_ref,
    b_in, w, wt, x, hg, bt,
    gbuf, pb, rs_send, rs_recv,
    ids, m1, col_a, line_a_out, line_a, col_b, line_b_out, line_b, z_b,
    u_out, u_in, line_d, col_d_out, col_d, line_u, col_u_out, col_u,
    ab, low, back_t, a_rows,
    in_sem, out_sem, ag_s, ag_r, rs_s, rs_r,
    ids_s, ids_r, ca_s, ca_r, la_s, la_r, cb_s, cb_r, lb_s, lb_r, zb_s, zb_r,
    zu_s, zu_r, ld_s, ld_r, cd_s, cd_r, lu_s, lu_r, cu_s, cu_r,
):
    rank, cols = b_in.shape
    width, tokens = x.shape
    features = w.shape[1]
    rows = tokens // 2
    half = cols // 2
    chunk = 256 if rows % 256 == 0 else rows
    d, z = lax.axis_index("dp"), lax.axis_index("mp")
    c = lax.rem(d, 2)
    y = lax.rem(lax.div(d, 2), ny)
    xx = lax.div(d, 2 * ny)
    line = xx * 2 + c

    def line_peer(o):
        other = lax.rem(line + o, nl)
        return ((lax.div(other, 2) * ny + y) * 2 + lax.rem(other, 2), z)

    def col_peer(o):
        return ((xx * ny + lax.rem(y + o, ny)) * 2 + c, z)

    def z_peer(o):
        return (d, lax.rem(z + o, nz))

    barrier = pltpu.get_barrier_semaphore()
    peers = [z_peer(o) for o in range(1, nz)]
    peers += [col_peer(o) for o in range(1, ny)]
    peers += [line_peer(o) for o in range(1, nl)]
    for peer in peers:
        pl.semaphore_signal(barrier, inc=1, device_id=peer, device_id_type=MESH)

    loads = []
    for i, (src, dst) in enumerate(
        ((g_hbm, gbuf.at[z]), (b_hbm, b_in), (a_hbm, col_a.at[pl.ds(0, rank), :]), (w_hbm, w), (x_hbm, x))
    ):
        copy = pltpu.make_async_copy(src, dst, in_sem.at[i])
        copy.start()
        loads.append(copy)

    pending = []

    def send(src, dst, send_sem, recv_sem, peer):
        copy = pltpu.make_async_remote_copy(
            src_ref=src, dst_ref=dst, send_sem=send_sem, recv_sem=recv_sem,
            device_id=peer, device_id_type=MESH,
        )
        copy.start()
        pending.append(copy)
        return copy

    def block(ref, o, size):
        return ref.at[pl.ds(o * size, size), :]

    def exchange(out, into, size, send_sem, recv_sem, peer, n, same=False):
        return [
            send(
                block(out, 0 if same else o, size), block(into, o, size),
                send_sem.at[o], recv_sem.at[o], peer(o),
            )
            for o in range(1, n)
        ]

    def arrive(copies):
        for copy in copies:
            copy.wait_recv()

    s0, s1 = tab_ref[idx_ref[0]], tab_ref[idx_ref[1]]
    row, lane = iota((8, 128), 0), iota((8, 128), 1)
    second = jnp.where(row == 2, lax.shift_right_logical(lane, 5) & 1, row & 1)
    ids[0:8, :] = jnp.where(second == 1, s1, s0)

    low_half = iota((1, 128), 1) < cols

    def swapped(v):
        return pltpu.roll(v, cols, 1)

    loads[1].wait()
    wide = onehot(iota((cols, 128), 0) == iota((cols, 128), 1))
    col_b[0:rank, :] = nn(b_in[...], wide).astype(BF16)
    loads[0].wait()
    loads[2].wait()
    pl.semaphore_wait(barrier, len(peers))

    most = nz // 2
    hops = ((most, most - 1), (most - 1, most))

    def toward(direction, n):
        return lax.rem(z + (n if direction == 0 else nz - n), nz)

    def ring_peer(direction):
        return (d, toward(direction, 1))

    ag = {}

    def ag_send(direction, h, t):
        part = gbuf.at[toward(1 - direction, t) if t else z, pl.ds(h * half, half), :]
        ag[direction, h, t] = send(
            part, part, ag_s.at[direction, h, t], ag_r.at[direction, h, t], ring_peer(direction)
        )

    served = set()

    def ag_serve(t):
        if t >= most or ("ag", t) in served:
            return
        served.add(("ag", t))
        for h in range(2):
            for direction in range(2):
                n = hops[direction][h]
                if t < n:
                    ag[direction, h, t].wait_recv()
                    if t + 1 < n:
                        ag_send(direction, h, t + 1)

    for h in range(2):
        for direction in range(2):
            if hops[direction][h]:
                ag_send(direction, h, 0)
    got_ids = exchange(ids, ids, 8, ids_s, ids_r, line_peer, nl, same=True)
    got_cb = exchange(col_b, col_b, rank, cb_s, cb_r, col_peer, ny, same=True)
    got_ca = exchange(col_a, col_a, rank, ca_s, ca_r, col_peer, ny, same=True)

    loads[3].wait()
    square = onehot(iota((features, features), 0) == iota((features, features), 1))
    wt[...] = nt(square, w[...]).astype(BF16)
    loads[4].wait()

    def base(step, carry):
        at = pl.ds(pl.multiple_of(step * chunk, chunk), chunk)
        part = nn(wt[...], x[:, at])
        for j in range(nz):
            pb[j, :, at] = part[j * cols : (j + 1) * cols, :]
        return carry

    lax.fori_loop(0, tokens // chunk, base, 0)

    arrive(got_ids)
    slot_in = (xx * ny + lax.rem(y + ny - lax.shift_right_logical(iota((rank, ny * rank), 1), 5), ny)) * 2 + c
    same_rank = (iota((rank, ny * rank), 1) & 31) == iota((rank, ny * rank), 0)
    for p in range(nl):
        q = (nl - p) % nl
        for s in range(2):
            own = ids[q * 8 + s : q * 8 + s + 1, :][:, 0:1]
            m1[(p * 2 + s) * rank : (p * 2 + s + 1) * rank, :] = onehot((slot_in == own) & same_rank)
    arrive(got_cb)
    line_b_out[...] = nn(m1[...], col_b[...]).astype(BF16)
    got_lb = exchange(line_b_out, line_b, 2 * rank, lb_s, lb_r, line_peer, nl)
    ag_serve(0)
    arrive(got_ca)
    line_a_out[...] = nn(m1[...], col_a[...]).astype(BF16)
    got_la = exchange(line_a_out, line_a, 2 * rank, la_s, la_r, line_peer, nl)

    def gathered(out, into, size, n):
        total = out[0:size, :].astype(F32)
        for o in range(1, n):
            total = total + into[o * size : (o + 1) * size, :].astype(F32)
        return total

    arrive(got_lb)
    mine = gathered(line_b_out, line_b, 2 * rank, nl)
    z_b[z] = (mine[0:rank, :] + swapped(mine[rank:, :])).astype(BF16)
    got_zb = [
        send(z_b.at[z], z_b.at[z], zb_s.at[o], zb_r.at[o], z_peer(o)) for o in range(1, nz)
    ]
    ag_serve(1)

    arrive(got_la)
    ab[...] = gathered(line_a_out, line_a, 2 * rank, nl).astype(BF16)
    for s in range(2):
        part = nn(ab[s * rank : (s + 1) * rank, :], x[:, s * rows : (s + 1) * rows])
        hi, rest = split(part)
        low[2 * s * rank : (2 * s + 1) * rank, :] = hi
        low[(2 * s + 1) * rank : (2 * s + 2) * rank, :] = rest
    ag_serve(2)
    arrive(got_zb)
    blocks = [z_b[j].astype(F32) for j in range(nz)]
    tiles = features // 128
    up = [
        [jnp.where(low_half, blocks[2 * i], swapped(blocks[2 * i + 1])) for i in range(tiles)],
        [jnp.where(low_half, swapped(blocks[2 * i]), blocks[2 * i + 1]) for i in range(tiles)],
    ]
    up = [jnp.concatenate(parts, axis=1).astype(BF16) for parts in up]
    for s in range(2):
        bt[s] = nt(square, jnp.concatenate([up[s], up[s]], axis=0)).astype(BF16)

        def adapt(step, carry):
            here = pl.ds(pl.multiple_of(step * chunk, chunk), chunk)
            at = pl.ds(pl.multiple_of(s * rows + step * chunk, chunk), chunk)
            part = nn(bt[s], low[2 * s * rank : 2 * (s + 1) * rank, here])
            for j in range(nz):
                pb[j, :, at] += part[j * cols : (j + 1) * cols, :]
            return carry

        lax.fori_loop(0, rows // chunk, adapt, 0)

    rs = {}

    def rs_go(direction, h, t):
        n = hops[direction][h]
        value = pb[toward(direction, n - t), h * half : (h + 1) * half, :]
        if t:
            value = value + rs_recv[direction, h, t - 1].astype(F32)
        rs_send[direction, h, t] = value.astype(BF16)
        rs[direction, h, t] = send(
            rs_send.at[direction, h, t], rs_recv.at[direction, h, t],
            rs_s.at[direction, h, t], rs_r.at[direction, h, t], ring_peer(direction),
        )

    def rs_serve(t):
        if t >= most or ("rs", t) in served:
            return
        served.add(("rs", t))
        for h in range(2):
            for direction in range(2):
                n = hops[direction][h]
                if t < n:
                    rs[direction, h, t].wait_recv()
                    if t + 1 < n:
                        rs_go(direction, h, t + 1)

    for h in range(2):
        for direction in range(2):
            if hops[direction][h]:
                rs_go(direction, h, 0)

    ag_serve(most - 1)

    def grads(s, at=None):
        at = pl.ds(s * rows, rows) if at is None else at
        return gbuf[:, :, at].reshape(nz * cols, at.size)

    ups = []
    for s in range(2):
        both = nt(low[2 * s * rank : 2 * (s + 1) * rank, :], grads(s))
        ups.append(both[0:rank, :] + both[rank:, :])
    for i in range(tiles):
        t0, t1 = (u[:, i * 128 : (i + 1) * 128] for u in ups)
        u_out[2 * i] = jnp.where(low_half, t0, swapped(t1)).astype(BF16)
        u_out[2 * i + 1] = jnp.where(low_half, swapped(t0), t1).astype(BF16)
    got_zu = [
        send(u_out.at[lax.rem(z + o, nz)], u_in.at[o], zu_s.at[o], zu_r.at[o], z_peer(o))
        for o in range(1, nz)
    ]
    for s in range(2):
        back_t[s * rank : (s + 1) * rank, :] = nn(up[s], grads(s)).astype(BF16)
        line_d[s * rank : (s + 1) * rank, :] = nt(
            back_t[s * rank : (s + 1) * rank, :], x[:, s * rows : (s + 1) * rows]
        ).astype(BF16)
    got_ld = exchange(line_d, line_d, 2 * rank, ld_s, ld_r, line_peer, nl, same=True)
    rs_serve(0)

    turn = onehot(iota((width, width), 0) == iota((width, width), 1))
    a_rows[...] = nt(turn, ab[...]).astype(BF16)

    def input_grad(s):
        def body(step, carry):
            here = pl.ds(pl.multiple_of(step * chunk, chunk), chunk)
            at = pl.ds(pl.multiple_of(s * rows + step * chunk, chunk), chunk)
            hg[:, at] = (
                nn(w[...], grads(s, at))
                + nn(a_rows[:, s * rank : (s + 1) * rank], back_t[s * rank : (s + 1) * rank, here])
            ).astype(BF16)
            return carry

        lax.fori_loop(0, rows // chunk, body, 0)
        at = pl.ds(s * rows, rows)
        copy = pltpu.make_async_copy(hg.at[:, at], hgrad_hbm.at[:, at], out_sem.at[s])
        copy.start()
        return copy

    stores = [input_grad(0)]
    arrive(got_zu)
    total = u_out[z].astype(F32)
    for o in range(1, nz):
        total = total + u_in[o].astype(F32)
    for s, part in enumerate((total, swapped(total))):
        line_u[s * rank : (s + 1) * rank, :] = jnp.where(low_half, part, 0.0).astype(BF16)
    got_lu = exchange(line_u, line_u, 2 * rank, lu_s, lu_r, line_peer, nl, same=True)
    rs_serve(1)

    arrive(got_ld)
    per_tile = 128 // (2 * rank)
    across = []
    for i in range(nl // per_tile):
        q = i * per_tile
        across.append(jnp.where(low_half, ids[q * 8 + 2 : q * 8 + 3, :], ids[q * 8 + 10 : q * 8 + 11, :]))
    across = jnp.concatenate(across, axis=1)
    shape = (ny * rank, nl * 2 * rank)
    slot_out = (xx * ny + lax.rem(y + lax.shift_right_logical(iota((ny * rank, 1), 0), 5), ny)) * 2 + c
    m2 = onehot((slot_out == across) & ((iota(shape, 1) & 31) == (iota(shape, 0) & 31)))
    summed = nn(m2, line_d[...])
    col_d_out[...] = summed.astype(BF16)
    got_cd = exchange(col_d_out, col_d, rank, cd_s, cd_r, col_peer, ny)
    own_d = summed[0:rank, :]
    arrive(got_lu)
    summed_u = nn(m2, line_u[...])
    col_u_out[...] = summed_u.astype(BF16)
    got_cu = exchange(col_u_out, col_u, rank, cu_s, cu_r, col_peer, ny)
    own_u = summed_u[0:rank, :]
    rs_serve(2)
    stores.append(input_grad(1))
    rs_serve(most - 1)
    for h in range(2):
        value = pb[z, h * half : (h + 1) * half, :]
        for direction in range(2):
            n = hops[direction][h]
            if n:
                value = value + rs_recv[direction, h, n - 1].astype(F32)
        values_ref[h * half : (h + 1) * half, :] = value.astype(BF16)

    arrive(got_cd)
    for o in range(1, ny):
        own_d = own_d + col_d[o * rank : (o + 1) * rank, :].astype(F32)
    down_ref[...] = own_d
    arrive(got_cu)
    for o in range(1, ny):
        own_u = own_u + col_u[o * rank : (o + 1) * rank, :].astype(F32)
    up_ref[...] = own_u[:, 0:cols]
    for copy in pending:
        copy.wait_send()
    for copy in stores:
        copy.wait()


def local(ny, nl, nz, hidden, weight, down, up, grad, index, table):
    tokens, width = hidden.shape
    rank = down.shape[2]
    cols = grad.shape[1]
    features = weight.shape[1]
    rows, half = tokens // 2, cols // 2
    most = nz // 2
    vm = pltpu.VMEM
    dma = pltpu.SemaphoreType.DMA
    scratch = [
        vm((rank, cols), BF16), vm((width, features), BF16), vm((features, width), BF16),
        vm((width, tokens), BF16), vm((width, tokens), BF16), vm((2, features, 2 * rank), BF16),
        vm((nz, cols, tokens), BF16), vm((nz, cols, tokens), F32),
        vm((2, 2, most, half, tokens), BF16), vm((2, 2, most, half, tokens), BF16),
        vm((8 * nl, 128), jnp.int32), vm((nl * 2 * rank, ny * rank), BF16),
        vm((ny * rank, width), BF16), vm((nl * 2 * rank, width), BF16), vm((nl * 2 * rank, width), BF16),
        vm((ny * rank, 128), BF16), vm((nl * 2 * rank, 128), BF16), vm((nl * 2 * rank, 128), BF16),
        vm((nz, rank, 128), BF16),
        vm((nz, rank, 128), BF16), vm((nz, rank, 128), BF16),
        vm((nl * 2 * rank, width), BF16), vm((ny * rank, width), BF16), vm((ny * rank, width), BF16),
        vm((nl * 2 * rank, 128), BF16), vm((ny * rank, 128), BF16), vm((ny * rank, 128), BF16),
        vm((2 * rank, width), BF16), vm((4 * rank, rows), BF16), vm((2 * rank, rows), BF16),
        vm((width, 2 * rank), BF16),
        dma((5,)), dma((2,)),
        dma((2, 2, most)), dma((2, 2, most)), dma((2, 2, most)), dma((2, 2, most)),
    ]
    for n in (nl, ny, nl, ny, nl, nz, nz, nl, ny, nl, ny):
        scratch += [dma((n,)), dma((n,))]
    anywhere = pl.BlockSpec(memory_space=pl.ANY)
    inside = pl.BlockSpec(memory_space=pltpu.VMEM)
    scalars = pl.BlockSpec(memory_space=pltpu.SMEM)
    values, hidden_grad, down_t, up_grad = pl.pallas_call(
        functools.partial(kernel, ny, nl, nz),
        out_shape=(
            jax.ShapeDtypeStruct((cols, tokens), BF16),
            jax.ShapeDtypeStruct((width, tokens), BF16),
            jax.ShapeDtypeStruct((rank, width), F32),
            jax.ShapeDtypeStruct((rank, cols), F32),
        ),
        in_specs=[scalars, scalars] + [anywhere] * 5,
        out_specs=(inside, anywhere, inside, inside),
        scratch_shapes=scratch,
        compiler_params=pltpu.CompilerParams(collective_id=0, has_side_effects=True),
        name="adapter_step",
    )(index, table, grad.T, up[0], down[0].T, weight, hidden.T)
    return values.T, hidden_grad.T, down_t.T[None], up_grad[None]


def build(mesh, ny):
    nl, nz = mesh.shape["dp"] // ny, mesh.shape["mp"]
    return jax.shard_map(
        functools.partial(local, ny, nl, nz),
        mesh=mesh,
        in_specs=(
            P("dp", "mp"),
            P("mp", None),
            P("dp", "mp", None),
            P("dp", None, "mp"),
            P("dp", "mp"),
            P("dp"),
            P(),
        ),
        out_specs=(P("dp", "mp"), P("dp", "mp"), P("dp", "mp", None), P("dp", None, "mp")),
        check_vma=False,
    )


def solution(mesh):
    return build(mesh, NY)
```

time: 312 us -> 67.9 us (0.22)
  waiting for transfers between devices: 159 us -> 0 us
  Pallas kernels: 0 us -> 61.7 us
  blocking collectives: 54.5 us -> 0 us
  local copies, waits for them, and re-layouts: 31.3 us -> 5.4 us
  starting transfers between devices: 19.8 us -> 0 us
  matrix products: 19.2 us -> 0 us
  between operations: 15.6 us -> 0.64 us
  other arithmetic: 11.3 us -> 0 us
    all_to_all x3 -> x0, waiting for transfers between devices: 93.4 us -> none  [the longest x2 48.1 us: from_everyone(): return lax.all_to_all(copies, axis, split_axis=0, concat_axis=0, tiled=True)]
    pallas_call x0 -> x1, Pallas kernels: none -> 61.7 us  [local(): pl.pallas_call(functools.partial(kernel, ny, nl, nz), out_shape=(jax.Shap...]
    all_gather x1 -> x0, blocking collectives: 54.5 us -> none  [local(): lax.all_gather(adapter_up_weight, 'dp', axis=0, tiled=True)]
    reduce_scatter x1 -> x0, waiting for transfers between devices: 40.3 us -> none  [local(): lax.psum_scatter(frozen_value_output, 'mp', scatter_dimension=1, tiled=True)]
    all_gather x2 -> x0, waiting for transfers between devices: 24.4 us -> none  [the longest x1 24.3 us: local(): lax.all_gather(adapter_down_weight, 'dp', axis=0, tiled=True)]
    all_to_all x3 -> x0, starting transfers between devices: 19.7 us -> none  [the longest x2 12.8 us: from_everyone(): return lax.all_to_all(copies, axis, split_axis=0, concat_axis=0, tiled=True)]
    dot_general x11 -> x0, matrix products: 18.1 us -> none  [the longest x1 3.9 us: local(): jnp.einsum('st,tdr->sdr', pick_half, down_all, preferred_element_type=jnp...]
    all_to_all x1 -> x0, local copies, waits for them, and re-layouts: 11.9 us -> none  [sent_together(): lax.all_to_all(both, axis, split_axis=split_dim, concat_axis=concat_dim,...]
  transfers between devices with their start and end apart: 6 -> 0, of which waited for: 5 -> 0; matrix products, arithmetic and copies ran while one was open for 17% -> 0% of each run, Pallas kernels for 0% -> 0%
where the time goes in v1:
time: 67.9 us; the launch traced here: 67.7 us
  Pallas kernels  61.7 us (91%)
  local copies, waits for them, and re-layouts  5.4 us (8%)
    pallas_call x1, Pallas kernels, local(): pl.pallas_call(functools.partial(kernel, ny, nl, nz), out_shape=(jax.Shap...  61.7 us
    unnamed x8, local copies, waits for them, and re-layouts  5.4 us

profile of v1, /device:TPU:1, one launch (start us, length us, event | category | flops | bytes accessed | tf_op | source)
XLA Modules:
  0.0 67.7 jit_solution(10849216772528218658)
XLA Ops:
  0.6 61.7 %adapter_step.1 = (bf16[64,1536]{1,0:T(8,128)(2,1)}, bf16[448,1536]{1,0:T(8,128)(2,1)}, f32[32,448]{1,0:T(8,128)}, f32[32,64]{1,0:T(8,128)}) custom-call(s32[2]{0:T(128)} %idx_ref.1, s32[64]{0:T(128)} %tab_ref.1, bf16[64,1536]{1,0:T(8,128)(2,1)} %bitcast.14, bf16[32,64]{1,0:T(8,128)(2,1)} %bitcast.19, bf16[32,448]{1,0:T(8,128)(2,1)} %bitcast.17, ...), custom_call_target="tpu_custom_call" | custom-call | tf_op jit(solution)/shard_map/adapter_step/pallas_call | solution.py:403
  62.3 1.6 %copy.15 = bf16[1536,64]{0,1:T(8,128)(2,1)} copy(bf16[1536,64]{0,1:T(8,128)(2,1)} %bitcast.15) | data formatting | bytes 393216
  63.9 0.0 copy-start
  63.9 0.0 copy-start.1
  63.9 2.5 %copy.16 = bf16[1536,448]{0,1:T(8,128)(2,1)} copy(bf16[1536,448]{0,1:T(8,128)(2,1)} %bitcast.13) | data formatting | bytes 2752512
  66.5 0.0 copy-done
  66.5 0.6 copy.17
  67.1 0.0 copy-done.1
  67.1 0.6 copy.18
Async XLA Ops:
  63.9 2.5 %copy-start = (f32[32,448]{1,0:T(8,128)S(1)}, f32[32,448]{1,0:T(8,128)}, u32[]{:S(2)}) copy-start(f32[32,448]{1,0:T(8,128)} %get-tuple-element.10) | copy-start | bytes 172036
  63.9 3.2 %copy-start.1 = (f32[32,64]{1,0:T(8,128)S(1)}, f32[32,64]{1,0:T(8,128)}, u32[]{:S(2)}) copy-start(f32[32,64]{1,0:T(8,128)} %get-tuple-element.11) | copy-start | bytes 24580

commit v2 on v1

--- a/solution.py
+++ b/solution.py
@@ -34,18 +34,22 @@
     return hi, (v - hi.astype(F32)).astype(BF16)
 
 
+def pieces(width):
+    first = (width // 2 + 127) // 128 * 128
+    return [(at, size) for at, size in ((0, first), (first, width - first)) if size]
+
+
 def kernel(
     ny, nl, nz,
-    idx_ref, tab_ref, g_hbm, b_hbm, a_hbm, w_hbm, x_hbm,
+    idx_hbm, tab_hbm, g_hbm, b_hbm, a_hbm, w_hbm, x_hbm,
     values_ref, hgrad_hbm, down_ref, up_ref,
-    b_in, w, wt, x, hg, bt,
+    idx_ref, tab_ref, b_in, w, wt, x, hg, bt,
     gbuf, pb, rs_send, rs_recv,
-    ids, m1, col_a, line_a_out, line_a, col_b, line_b_out, line_b, z_b,
-    u_out, u_in, line_d, col_d_out, col_d, line_u, col_u_out, col_u,
-    ab, low, back_t, a_rows,
+    ids, m1, m2, col_b, line_b_out, line_b, z_b, u_out, u_in, line_u, col_u_out, col_u,
+    low, back_t, a_rows,
     in_sem, out_sem, ag_s, ag_r, rs_s, rs_r,
-    ids_s, ids_r, ca_s, ca_r, la_s, la_r, cb_s, cb_r, lb_s, lb_r, zb_s, zb_r,
-    zu_s, zu_r, ld_s, ld_r, cd_s, cd_r, lu_s, lu_r, cu_s, cu_r,
+    ids_s, ids_r, cb_s, cb_r, lb_s, lb_r, zb_s, zb_r, zu_s, zu_r, lu_s, lu_r, cu_s, cu_r,
+    *by_piece,
 ):
     rank, cols = b_in.shape
     width, tokens = x.shape
@@ -53,6 +57,12 @@
     rows = tokens // 2
     half = cols // 2
     chunk = 256 if rows % 256 == 0 else rows
+    cuts = pieces(width)
+    parts = range(len(cuts))
+    col_a, line_a_out, line_a, ab, line_d, col_d_out, col_d = (
+        by_piece[i * len(cuts) : (i + 1) * len(cuts)] for i in range(7)
+    )
+    ca_s, ca_r, la_s, la_r, ld_s, ld_r, cd_s, cd_r = by_piece[7 * len(cuts) :]
     d, z = lax.axis_index("dp"), lax.axis_index("mp")
     c = lax.rem(d, 2)
     y = lax.rem(lax.div(d, 2), ny)
@@ -77,9 +87,10 @@
         pl.semaphore_signal(barrier, inc=1, device_id=peer, device_id_type=MESH)
 
     loads = []
-    for i, (src, dst) in enumerate(
-        ((g_hbm, gbuf.at[z]), (b_hbm, b_in), (a_hbm, col_a.at[pl.ds(0, rank), :]), (w_hbm, w), (x_hbm, x))
-    ):
+    wanted = [(idx_hbm, idx_ref), (tab_hbm, tab_ref), (g_hbm, gbuf.at[z]), (b_hbm, b_in)]
+    wanted += [(a_hbm.at[:, pl.ds(*cuts[p])], col_a[p].at[pl.ds(0, rank), :]) for p in parts]
+    wanted += [(w_hbm, w), (x_hbm, x)]
+    for i, (src, dst) in enumerate(wanted):
         copy = pltpu.make_async_copy(src, dst, in_sem.at[i])
         copy.start()
         loads.append(copy)
@@ -111,6 +122,8 @@
         for copy in copies:
             copy.wait_recv()
 
+    loads[0].wait()
+    loads[1].wait()
     s0, s1 = tab_ref[idx_ref[0]], tab_ref[idx_ref[1]]
     row, lane = iota((8, 128), 0), iota((8, 128), 1)
     second = jnp.where(row == 2, lax.shift_right_logical(lane, 5) & 1, row & 1)
@@ -121,11 +134,12 @@
     def swapped(v):
         return pltpu.roll(v, cols, 1)
 
-    loads[1].wait()
+    loads[3].wait()
     wide = onehot(iota((cols, 128), 0) == iota((cols, 128), 1))
     col_b[0:rank, :] = nn(b_in[...], wide).astype(BF16)
-    loads[0].wait()
     loads[2].wait()
+    for p in parts:
+        loads[4 + p].wait()
     pl.semaphore_wait(barrier, len(peers))
 
     most = nz // 2
@@ -147,11 +161,11 @@
 
     served = set()
 
-    def ag_serve(t):
-        if t >= most or ("ag", t) in served:
-            return
-        served.add(("ag", t))
-        for h in range(2):
+    def ag_serve(t, *halves):
+        for h in halves:
+            if ("ag", t, h) in served:
+                continue
+            served.add(("ag", t, h))
             for direction in range(2):
                 n = hops[direction][h]
                 if t < n:
@@ -165,12 +179,14 @@
                 ag_send(direction, h, 0)
     got_ids = exchange(ids, ids, 8, ids_s, ids_r, line_peer, nl, same=True)
     got_cb = exchange(col_b, col_b, rank, cb_s, cb_r, col_peer, ny, same=True)
-    got_ca = exchange(col_a, col_a, rank, ca_s, ca_r, col_peer, ny, same=True)
-
-    loads[3].wait()
+    got_ca = [
+        exchange(col_a[p], col_a[p], rank, ca_s.at[p], ca_r.at[p], col_peer, ny, same=True) for p in parts
+    ]
+
+    loads[-2].wait()
     square = onehot(iota((features, features), 0) == iota((features, features), 1))
     wt[...] = nt(square, w[...]).astype(BF16)
-    loads[4].wait()
+    loads[-1].wait()
 
     def base(step, carry):
         at = pl.ds(pl.multiple_of(step * chunk, chunk), chunk)
@@ -189,36 +205,33 @@
         for s in range(2):
             own = ids[q * 8 + s : q * 8 + s + 1, :][:, 0:1]
             m1[(p * 2 + s) * rank : (p * 2 + s + 1) * rank, :] = onehot((slot_in == own) & same_rank)
-    arrive(got_cb)
-    line_b_out[...] = nn(m1[...], col_b[...]).astype(BF16)
-    got_lb = exchange(line_b_out, line_b, 2 * rank, lb_s, lb_r, line_peer, nl)
-    ag_serve(0)
-    arrive(got_ca)
-    line_a_out[...] = nn(m1[...], col_a[...]).astype(BF16)
-    got_la = exchange(line_a_out, line_a, 2 * rank, la_s, la_r, line_peer, nl)
-
     def gathered(out, into, size, n):
         total = out[0:size, :].astype(F32)
         for o in range(1, n):
             total = total + into[o * size : (o + 1) * size, :].astype(F32)
         return total
 
+    def pick_a(p):
+        arrive(got_ca[p])
+        line_a_out[p][...] = nn(m1[...], col_a[p][...]).astype(BF16)
+        return exchange(line_a_out[p], line_a[p], 2 * rank, la_s.at[p], la_r.at[p], line_peer, nl)
+
+    ag_serve(0, 0)
+    arrive(got_cb)
+    line_b_out[...] = nn(m1[...], col_b[...]).astype(BF16)
+    got_lb = exchange(line_b_out, line_b, 2 * rank, lb_s, lb_r, line_peer, nl)
+    got_la = [pick_a(0)]
+    ag_serve(0, 1)
     arrive(got_lb)
     mine = gathered(line_b_out, line_b, 2 * rank, nl)
     z_b[z] = (mine[0:rank, :] + swapped(mine[rank:, :])).astype(BF16)
     got_zb = [
         send(z_b.at[z], z_b.at[z], zb_s.at[o], zb_r.at[o], z_peer(o)) for o in range(1, nz)
     ]
-    ag_serve(1)
-
-    arrive(got_la)
-    ab[...] = gathered(line_a_out, line_a, 2 * rank, nl).astype(BF16)
-    for s in range(2):
-        part = nn(ab[s * rank : (s + 1) * rank, :], x[:, s * rows : (s + 1) * rows])
-        hi, rest = split(part)
-        low[2 * s * rank : (2 * s + 1) * rank, :] = hi
-        low[(2 * s + 1) * rank : (2 * s + 2) * rank, :] = rest
-    ag_serve(2)
+    ag_serve(1, 0)
+    got_la += [pick_a(p) for p in parts[1:]]
+    ag_serve(1, 1)
+    ag_serve(2, 0)
     arrive(got_zb)
     blocks = [z_b[j].astype(F32) for j in range(nz)]
     tiles = features // 128
@@ -230,6 +243,21 @@
     for s in range(2):
         bt[s] = nt(square, jnp.concatenate([up[s], up[s]], axis=0)).astype(BF16)
 
+    ag_serve(2, 1)
+    for p in parts:
+        arrive(got_la[p])
+        ab[p][...] = gathered(line_a_out[p], line_a[p], 2 * rank, nl).astype(BF16)
+    for s in range(2):
+        part = 0.0
+        for p in parts:
+            at, size = cuts[p]
+            part = part + nn(ab[p][s * rank : (s + 1) * rank, :], x[at : at + size, s * rows : (s + 1) * rows])
+        hi, rest = split(part)
+        low[2 * s * rank : (2 * s + 1) * rank, :] = hi
+        low[(2 * s + 1) * rank : (2 * s + 2) * rank, :] = rest
+
+    for s in range(2):
+
         def adapt(step, carry):
             here = pl.ds(pl.multiple_of(step * chunk, chunk), chunk)
             at = pl.ds(pl.multiple_of(s * rows + step * chunk, chunk), chunk)
@@ -253,11 +281,11 @@
             rs_s.at[direction, h, t], rs_r.at[direction, h, t], ring_peer(direction),
         )
 
-    def rs_serve(t):
-        if t >= most or ("rs", t) in served:
-            return
-        served.add(("rs", t))
-        for h in range(2):
+    def rs_serve(t, *halves):
+        for h in halves:
+            if ("rs", t, h) in served:
+                continue
+            served.add(("rs", t, h))
             for direction in range(2):
                 n = hops[direction][h]
                 if t < n:
@@ -270,12 +298,25 @@
             if hops[direction][h]:
                 rs_go(direction, h, 0)
 
-    ag_serve(most - 1)
+    for t in range(most):
+        ag_serve(t, 0, 1)
 
     def grads(s, at=None):
         at = pl.ds(s * rows, rows) if at is None else at
         return gbuf[:, :, at].reshape(nz * cols, at.size)
 
+    got_ld = []
+    for s in range(2):
+        back_t[s * rank : (s + 1) * rank, :] = nn(up[s], grads(s)).astype(BF16)
+    for p in parts:
+        at, size = cuts[p]
+        for s in range(2):
+            line_d[p][s * rank : (s + 1) * rank, :] = nt(
+                back_t[s * rank : (s + 1) * rank, :], x[at : at + size, s * rows : (s + 1) * rows]
+            ).astype(BF16)
+        got_ld.append(
+            exchange(line_d[p], line_d[p], 2 * rank, ld_s.at[p], ld_r.at[p], line_peer, nl, same=True)
+        )
     ups = []
     for s in range(2):
         both = nt(low[2 * s * rank : 2 * (s + 1) * rank, :], grads(s))
@@ -288,16 +329,19 @@
         send(u_out.at[lax.rem(z + o, nz)], u_in.at[o], zu_s.at[o], zu_r.at[o], z_peer(o))
         for o in range(1, nz)
     ]
-    for s in range(2):
-        back_t[s * rank : (s + 1) * rank, :] = nn(up[s], grads(s)).astype(BF16)
-        line_d[s * rank : (s + 1) * rank, :] = nt(
-            back_t[s * rank : (s + 1) * rank, :], x[:, s * rows : (s + 1) * rows]
-        ).astype(BF16)
-    got_ld = exchange(line_d, line_d, 2 * rank, ld_s, ld_r, line_peer, nl, same=True)
-    rs_serve(0)
-
-    turn = onehot(iota((width, width), 0) == iota((width, width), 1))
-    a_rows[...] = nt(turn, ab[...]).astype(BF16)
+    per_tile = 128 // (2 * rank)
+    across = []
+    for i in range(nl // per_tile):
+        q = i * per_tile
+        across.append(jnp.where(low_half, ids[q * 8 + 2 : q * 8 + 3, :], ids[q * 8 + 10 : q * 8 + 11, :]))
+    across = jnp.concatenate(across, axis=1)
+    shape = (ny * rank, nl * 2 * rank)
+    slot_out = (xx * ny + lax.rem(y + lax.shift_right_logical(iota((ny * rank, 1), 0), 5), ny)) * 2 + c
+    m2[...] = onehot((slot_out == across) & ((iota(shape, 1) & 31) == (iota(shape, 0) & 31)))
+    for p in parts:
+        at, size = cuts[p]
+        turn = onehot(iota((size, size), 0) == iota((size, size), 1))
+        a_rows[at : at + size, :] = nt(turn, ab[p][...]).astype(BF16)
 
     def input_grad(s):
         def body(step, carry):
@@ -315,7 +359,21 @@
         copy.start()
         return copy
 
+    rs_serve(0, 0)
     stores = [input_grad(0)]
+    rs_serve(0, 1)
+    got_cd, own_d = [], []
+
+    def spread_d(p):
+        arrive(got_ld[p])
+        summed = nn(m2[...], line_d[p][...])
+        col_d_out[p][...] = summed.astype(BF16)
+        got_cd.append(
+            exchange(col_d_out[p], col_d[p], rank, cd_s.at[p], cd_r.at[p], col_peer, ny)
+        )
+        own_d.append(summed[0:rank, :])
+
+    spread_d(0)
     arrive(got_zu)
     total = u_out[z].astype(F32)
     for o in range(1, nz):
@@ -323,30 +381,19 @@
     for s, part in enumerate((total, swapped(total))):
         line_u[s * rank : (s + 1) * rank, :] = jnp.where(low_half, part, 0.0).astype(BF16)
     got_lu = exchange(line_u, line_u, 2 * rank, lu_s, lu_r, line_peer, nl, same=True)
-    rs_serve(1)
-
-    arrive(got_ld)
-    per_tile = 128 // (2 * rank)
-    across = []
-    for i in range(nl // per_tile):
-        q = i * per_tile
-        across.append(jnp.where(low_half, ids[q * 8 + 2 : q * 8 + 3, :], ids[q * 8 + 10 : q * 8 + 11, :]))
-    across = jnp.concatenate(across, axis=1)
-    shape = (ny * rank, nl * 2 * rank)
-    slot_out = (xx * ny + lax.rem(y + lax.shift_right_logical(iota((ny * rank, 1), 0), 5), ny)) * 2 + c
-    m2 = onehot((slot_out == across) & ((iota(shape, 1) & 31) == (iota(shape, 0) & 31)))
-    summed = nn(m2, line_d[...])
-    col_d_out[...] = summed.astype(BF16)
-    got_cd = exchange(col_d_out, col_d, rank, cd_s, cd_r, col_peer, ny)
-    own_d = summed[0:rank, :]
+    rs_serve(1, 0)
+    for p in parts[1:]:
+        spread_d(p)
+    rs_serve(1, 1)
     arrive(got_lu)
-    summed_u = nn(m2, line_u[...])
+    summed_u = nn(m2[...], line_u[...])
     col_u_out[...] = summed_u.astype(BF16)
     got_cu = exchange(col_u_out, col_u, rank, cu_s, cu_r, col_peer, ny)
     own_u = summed_u[0:rank, :]
-    rs_serve(2)
     stores.append(input_grad(1))
-    rs_serve(most - 1)
+    for t in range(2, most):
+        rs_serve(t, 0)
+        rs_serve(t, 1)
     for h in range(2):
         value = pb[z, h * half : (h + 1) * half, :]
         for direction in range(2):
@@ -355,10 +402,11 @@
                 value = value + rs_recv[direction, h, n - 1].astype(F32)
         values_ref[h * half : (h + 1) * half, :] = value.astype(BF16)
 
-    arrive(got_cd)
-    for o in range(1, ny):
-        own_d = own_d + col_d[o * rank : (o + 1) * rank, :].astype(F32)
-    down_ref[...] = own_d
+    for p in parts:
+        arrive(got_cd[p])
+        for o in range(1, ny):
+            own_d[p] = own_d[p] + col_d[p][o * rank : (o + 1) * rank, :].astype(F32)
+        down_ref[:, cuts[p][0] : cuts[p][0] + cuts[p][1]] = own_d[p]
     arrive(got_cu)
     for o in range(1, ny):
         own_u = own_u + col_u[o * rank : (o + 1) * rank, :].astype(F32)
@@ -366,6 +414,26 @@
     for copy in pending:
         copy.wait_send()
     for copy in stores:
+        copy.wait()
+
+
+def place_results(*refs):
+    sources, results, held, sems = refs[:4], refs[4:8], refs[8:12], refs[12]
+    jobs = []
+    for source, result, via in zip(sources, results, held):
+        size = source.shape[0] // (4 if source.shape[0] % 64 == 0 else 1)
+        jobs += [
+            tuple(ref.at[pl.ds(at, size), :] for ref in (source, via, result))
+            for at in range(0, source.shape[0], size)
+        ]
+    into = [pltpu.make_async_copy(s, v, sems.at[0, i]) for i, (s, v, _) in enumerate(jobs)]
+    out = [pltpu.make_async_copy(v, r, sems.at[1, i]) for i, (_, v, r) in enumerate(jobs)]
+    for copy in into:
+        copy.start()
+    for first, second in zip(into, out):
+        first.wait()
+        second.start()
+    for copy in out:
         copy.wait()
 
 
@@ -378,28 +446,30 @@
     most = nz // 2
     vm = pltpu.VMEM
     dma = pltpu.SemaphoreType.DMA
+    cuts = pieces(width)
     scratch = [
+        pltpu.SMEM(index.shape, jnp.int32), pltpu.SMEM(table.shape, jnp.int32),
         vm((rank, cols), BF16), vm((width, features), BF16), vm((features, width), BF16),
         vm((width, tokens), BF16), vm((width, tokens), BF16), vm((2, features, 2 * rank), BF16),
         vm((nz, cols, tokens), BF16), vm((nz, cols, tokens), F32),
         vm((2, 2, most, half, tokens), BF16), vm((2, 2, most, half, tokens), BF16),
-        vm((8 * nl, 128), jnp.int32), vm((nl * 2 * rank, ny * rank), BF16),
-        vm((ny * rank, width), BF16), vm((nl * 2 * rank, width), BF16), vm((nl * 2 * rank, width), BF16),
+        vm((8 * nl, 128), jnp.int32),
+        vm((nl * 2 * rank, ny * rank), BF16), vm((ny * rank, nl * 2 * rank), BF16),
         vm((ny * rank, 128), BF16), vm((nl * 2 * rank, 128), BF16), vm((nl * 2 * rank, 128), BF16),
-        vm((nz, rank, 128), BF16),
-        vm((nz, rank, 128), BF16), vm((nz, rank, 128), BF16),
-        vm((nl * 2 * rank, width), BF16), vm((ny * rank, width), BF16), vm((ny * rank, width), BF16),
+        vm((nz, rank, 128), BF16), vm((nz, rank, 128), BF16), vm((nz, rank, 128), BF16),
         vm((nl * 2 * rank, 128), BF16), vm((ny * rank, 128), BF16), vm((ny * rank, 128), BF16),
-        vm((2 * rank, width), BF16), vm((4 * rank, rows), BF16), vm((2 * rank, rows), BF16),
-        vm((width, 2 * rank), BF16),
-        dma((5,)), dma((2,)),
+        vm((4 * rank, rows), BF16), vm((2 * rank, rows), BF16), vm((width, 2 * rank), BF16),
+        dma((6 + len(cuts),)), dma((2,)),
         dma((2, 2, most)), dma((2, 2, most)), dma((2, 2, most)), dma((2, 2, most)),
     ]
-    for n in (nl, ny, nl, ny, nl, nz, nz, nl, ny, nl, ny):
+    for n in (nl, ny, nl, nz, nz, nl, ny):
         scratch += [dma((n,)), dma((n,))]
+    for n in (ny, 2 * nl, 2 * nl, 2, 2 * nl, ny, ny):
+        scratch += [vm((n * rank, size), BF16) for _, size in cuts]
+    for n in (ny, nl, nl, ny):
+        scratch += [dma((len(cuts), n)), dma((len(cuts), n))]
     anywhere = pl.BlockSpec(memory_space=pl.ANY)
     inside = pl.BlockSpec(memory_space=pltpu.VMEM)
-    scalars = pl.BlockSpec(memory_space=pltpu.SMEM)
     values, hidden_grad, down_t, up_grad = pl.pallas_call(
         functools.partial(kernel, ny, nl, nz),
         out_shape=(
@@ -408,12 +478,21 @@
             jax.ShapeDtypeStruct((rank, width), F32),
             jax.ShapeDtypeStruct((rank, cols), F32),
         ),
-        in_specs=[scalars, scalars] + [anywhere] * 5,
+        in_specs=[pl.BlockSpec(memory_space=pltpu.HBM)] * 7,
         out_specs=(inside, anywhere, inside, inside),
         scratch_shapes=scratch,
         compiler_params=pltpu.CompilerParams(collective_id=0, has_side_effects=True),
         name="adapter_step",
     )(index, table, grad.T, up[0], down[0].T, weight, hidden.T)
+    results = (values, hidden_grad, down_t, up_grad)
+    values, hidden_grad, down_t, up_grad = pl.pallas_call(
+        place_results,
+        out_shape=tuple(jax.ShapeDtypeStruct(r.shape, r.dtype) for r in results),
+        in_specs=[anywhere] * 4,
+        out_specs=(pl.BlockSpec(memory_space=pltpu.HBM),) * 4,
+        scratch_shapes=[vm(r.shape, r.dtype) for r in results] + [dma((2, 16))],
+        name="place_results",
+    )(*results)
     return values.T, hidden_grad.T, down_t.T[None], up_grad[None]
 
 

time: 67.9 us -> 63.7 us (0.938)
  local copies, waits for them, and re-layouts: 5.4 us -> 0 us
  Pallas kernels: 61.7 us -> 62.9 us
    unnamed x8 -> x0, local copies, waits for them, and re-layouts: 5.4 us -> none
    pallas_call x0 -> x1, Pallas kernels: none -> 2.46 us  [local(): pl.pallas_call(place_results, out_shape=tuple((jax.ShapeDtypeStruct(r.sha...]
    pallas_call x1, Pallas kernels: 61.7 us -> 60.4 us  [local(): pl.pallas_call(functools.partial(kernel, ny, nl, nz), out_shape=(jax.Shap...]
where the time goes in v2:
time: 63.7 us; the launch traced here: 63.5 us
  Pallas kernels  62.9 us (99%)
  between operations  0.64 us (1%)
    pallas_call x1, Pallas kernels, local(): pl.pallas_call(functools.partial(kernel, ny, nl, nz), out_shape=(jax.Shap...  60.4 us
    pallas_call x1, Pallas kernels, local(): pl.pallas_call(place_results, out_shape=tuple((jax.ShapeDtypeStruct(r.sha...  2.46 us

profile of v2, /device:TPU:1, one launch (start us, length us, event | category | flops | bytes accessed | tf_op | source)
XLA Modules:
  0.0 63.5 jit_solution(7677673967793869760)
XLA Ops:
  0.6 60.4 %adapter_step.1 = (bf16[64,1536]{1,0:T(8,128)(2,1)}, bf16[448,1536]{1,0:T(8,128)(2,1)}, f32[32,448]{1,0:T(8,128)}, f32[32,64]{1,0:T(8,128)}) custom-call(s32[2]{0:T(128)} %idx_hbm.1, s32[64]{0:T(128)} %tab_hbm.1, bf16[64,1536]{1,0:T(8,128)(2,1)} %bitcast.13, bf16[32,64]{1,0:T(8,128)(2,1)} %bitcast.15, bf16[32,448]{1,0:T(8,128)(2,1)} %bitcast.14, ...), custom_call_target="tpu_custom_call" | custom-call | tf_op jit(solution)/shard_map/adapter_step/pallas_call | solution.py:473
  61.1 2.5 %place_results.1 = (bf16[64,1536]{1,0:T(8,128)(2,1)}, bf16[448,1536]{1,0:T(8,128)(2,1)}, f32[32,448]{1,0:T(8,128)}, f32[32,64]{1,0:T(8,128)}) custom-call(bf16[64,1536]{1,0:T(8,128)(2,1)} %get-tuple-element.12.refs_0_, bf16[448,1536]{1,0:T(8,128)(2,1)} %get-tuple-element.13.refs_1_, f32[32,448]{1,0:T(8,128)} %get-tuple-element.14.refs_2_, ...), custom_call_target="tpu_custom_call" | custom-call | tf_op jit(solution)/shard_map/place_results/pallas_call | solution.py:488

commit v3 on v2

--- a/solution.py
+++ b/solution.py
@@ -10,6 +10,7 @@
 F32 = jnp.float32
 BF16 = jnp.bfloat16
 MESH = pl.DeviceIdType.MESH
+QUARTERS = 4
 NY = 8
 
 
@@ -55,7 +56,7 @@
     width, tokens = x.shape
     features = w.shape[1]
     rows = tokens // 2
-    half = cols // 2
+    part_rows = cols // QUARTERS
     chunk = 256 if rows % 256 == 0 else rows
     cuts = pieces(width)
     parts = range(len(cuts))
@@ -143,7 +144,7 @@
     pl.semaphore_wait(barrier, len(peers))
 
     most = nz // 2
-    hops = ((most, most - 1), (most - 1, most))
+    hops = [[most - ((h < QUARTERS // 2) == bool(side)) for h in range(QUARTERS)] for side in range(2)]
 
     def toward(direction, n):
         return lax.rem(z + (n if direction == 0 else nz - n), nz)
@@ -154,15 +155,15 @@
     ag = {}
 
     def ag_send(direction, h, t):
-        part = gbuf.at[toward(1 - direction, t) if t else z, pl.ds(h * half, half), :]
+        part = gbuf.at[toward(1 - direction, t) if t else z, pl.ds(h * part_rows, part_rows), :]
         ag[direction, h, t] = send(
             part, part, ag_s.at[direction, h, t], ag_r.at[direction, h, t], ring_peer(direction)
         )
 
     served = set()
 
-    def ag_serve(t, *halves):
-        for h in halves:
+    def ag_serve(t, *sides):
+        for h in [h for h in range(QUARTERS) if h * 2 // QUARTERS in sides]:
             if ("ag", t, h) in served:
                 continue
             served.add(("ag", t, h))
@@ -173,7 +174,7 @@
                     if t + 1 < n:
                         ag_send(direction, h, t + 1)
 
-    for h in range(2):
+    for h in range(QUARTERS):
         for direction in range(2):
             if hops[direction][h]:
                 ag_send(direction, h, 0)
@@ -232,18 +233,6 @@
     got_la += [pick_a(p) for p in parts[1:]]
     ag_serve(1, 1)
     ag_serve(2, 0)
-    arrive(got_zb)
-    blocks = [z_b[j].astype(F32) for j in range(nz)]
-    tiles = features // 128
-    up = [
-        [jnp.where(low_half, blocks[2 * i], swapped(blocks[2 * i + 1])) for i in range(tiles)],
-        [jnp.where(low_half, swapped(blocks[2 * i]), blocks[2 * i + 1]) for i in range(tiles)],
-    ]
-    up = [jnp.concatenate(parts, axis=1).astype(BF16) for parts in up]
-    for s in range(2):
-        bt[s] = nt(square, jnp.concatenate([up[s], up[s]], axis=0)).astype(BF16)
-
-    ag_serve(2, 1)
     for p in parts:
         arrive(got_la[p])
         ab[p][...] = gathered(line_a_out[p], line_a[p], 2 * rank, nl).astype(BF16)
@@ -256,23 +245,31 @@
         low[2 * s * rank : (2 * s + 1) * rank, :] = hi
         low[(2 * s + 1) * rank : (2 * s + 2) * rank, :] = rest
 
+    ag_serve(2, 1)
+    arrive(got_zb)
+    blocks = [z_b[j].astype(F32) for j in range(nz)]
+    tiles = features // 128
+    up = [
+        [jnp.where(low_half, blocks[2 * i], swapped(blocks[2 * i + 1])) for i in range(tiles)],
+        [jnp.where(low_half, swapped(blocks[2 * i]), blocks[2 * i + 1]) for i in range(tiles)],
+    ]
+    up = [jnp.concatenate(parts, axis=1).astype(BF16) for parts in up]
     for s in range(2):
-
-        def adapt(step, carry):
-            here = pl.ds(pl.multiple_of(step * chunk, chunk), chunk)
-            at = pl.ds(pl.multiple_of(s * rows + step * chunk, chunk), chunk)
-            part = nn(bt[s], low[2 * s * rank : 2 * (s + 1) * rank, here])
-            for j in range(nz):
-                pb[j, :, at] += part[j * cols : (j + 1) * cols, :]
-            return carry
-
-        lax.fori_loop(0, rows // chunk, adapt, 0)
+        turned = nt(square, jnp.concatenate([up[s], up[s]], axis=0)).astype(BF16)
+        bt[s] = turned.reshape(nz, cols, 2 * rank)
+
+    def contribution(j, h):
+        at = slice(h * part_rows, (h + 1) * part_rows)
+        adapted = [
+            nn(bt[s, j, at, :], low[2 * s * rank : 2 * (s + 1) * rank, :]) for s in range(2)
+        ]
+        return pb[j, at, :] + jnp.concatenate(adapted, axis=1)
 
     rs = {}
 
     def rs_go(direction, h, t):
         n = hops[direction][h]
-        value = pb[toward(direction, n - t), h * half : (h + 1) * half, :]
+        value = contribution(toward(direction, n - t), h)
         if t:
             value = value + rs_recv[direction, h, t - 1].astype(F32)
         rs_send[direction, h, t] = value.astype(BF16)
@@ -281,8 +278,8 @@
             rs_s.at[direction, h, t], rs_r.at[direction, h, t], ring_peer(direction),
         )
 
-    def rs_serve(t, *halves):
-        for h in halves:
+    def rs_serve(t, *sides):
+        for h in [h for h in range(QUARTERS) if h * 2 // QUARTERS in sides]:
             if ("rs", t, h) in served:
                 continue
             served.add(("rs", t, h))
@@ -293,7 +290,7 @@
                     if t + 1 < n:
                         rs_go(direction, h, t + 1)
 
-    for h in range(2):
+    for h in range(QUARTERS):
         for direction in range(2):
             if hops[direction][h]:
                 rs_go(direction, h, 0)
@@ -394,13 +391,13 @@
     for t in range(2, most):
         rs_serve(t, 0)
         rs_serve(t, 1)
-    for h in range(2):
-        value = pb[z, h * half : (h + 1) * half, :]
+    for h in range(QUARTERS):
+        value = contribution(z, h)
         for direction in range(2):
             n = hops[direction][h]
             if n:
                 value = value + rs_recv[direction, h, n - 1].astype(F32)
-        values_ref[h * half : (h + 1) * half, :] = value.astype(BF16)
+        values_ref[h * part_rows : (h + 1) * part_rows, :] = value.astype(BF16)
 
     for p in parts:
         arrive(got_cd[p])
@@ -418,22 +415,11 @@
 
 
 def place_results(*refs):
-    sources, results, held, sems = refs[:4], refs[4:8], refs[8:12], refs[12]
-    jobs = []
-    for source, result, via in zip(sources, results, held):
-        size = source.shape[0] // (4 if source.shape[0] % 64 == 0 else 1)
-        jobs += [
-            tuple(ref.at[pl.ds(at, size), :] for ref in (source, via, result))
-            for at in range(0, source.shape[0], size)
-        ]
-    into = [pltpu.make_async_copy(s, v, sems.at[0, i]) for i, (s, v, _) in enumerate(jobs)]
-    out = [pltpu.make_async_copy(v, r, sems.at[1, i]) for i, (_, v, r) in enumerate(jobs)]
-    for copy in into:
+    sem = refs[8]
+    copies = [pltpu.make_async_copy(refs[i], refs[4 + i], sem.at[i]) for i in range(4)]
+    for copy in copies:
         copy.start()
-    for first, second in zip(into, out):
-        first.wait()
-        second.start()
-    for copy in out:
+    for copy in copies:
         copy.wait()
 
 
@@ -442,7 +428,7 @@
     rank = down.shape[2]
     cols = grad.shape[1]
     features = weight.shape[1]
-    rows, half = tokens // 2, cols // 2
+    rows, part_rows = tokens // 2, cols // QUARTERS
     most = nz // 2
     vm = pltpu.VMEM
     dma = pltpu.SemaphoreType.DMA
@@ -450,9 +436,9 @@
     scratch = [
         pltpu.SMEM(index.shape, jnp.int32), pltpu.SMEM(table.shape, jnp.int32),
         vm((rank, cols), BF16), vm((width, features), BF16), vm((features, width), BF16),
-        vm((width, tokens), BF16), vm((width, tokens), BF16), vm((2, features, 2 * rank), BF16),
+        vm((width, tokens), BF16), vm((width, tokens), BF16), vm((2, nz, cols, 2 * rank), BF16),
         vm((nz, cols, tokens), BF16), vm((nz, cols, tokens), F32),
-        vm((2, 2, most, half, tokens), BF16), vm((2, 2, most, half, tokens), BF16),
+        vm((2, QUARTERS, most, part_rows, tokens), BF16), vm((2, QUARTERS, most, part_rows, tokens), BF16),
         vm((8 * nl, 128), jnp.int32),
         vm((nl * 2 * rank, ny * rank), BF16), vm((ny * rank, nl * 2 * rank), BF16),
         vm((ny * rank, 128), BF16), vm((nl * 2 * rank, 128), BF16), vm((nl * 2 * rank, 128), BF16),
@@ -460,7 +446,7 @@
         vm((nl * 2 * rank, 128), BF16), vm((ny * rank, 128), BF16), vm((ny * rank, 128), BF16),
         vm((4 * rank, rows), BF16), vm((2 * rank, rows), BF16), vm((width, 2 * rank), BF16),
         dma((6 + len(cuts),)), dma((2,)),
-        dma((2, 2, most)), dma((2, 2, most)), dma((2, 2, most)), dma((2, 2, most)),
+        *([dma((2, QUARTERS, most))] * 4),
     ]
     for n in (nl, ny, nl, nz, nz, nl, ny):
         scratch += [dma((n,)), dma((n,))]
@@ -473,15 +459,12 @@
     values, hidden_grad, down_t, up_grad = pl.pallas_call(
         functools.partial(kernel, ny, nl, nz),
         out_shape=(
-            jax.ShapeDtypeStruct((cols, tokens), BF16),
-            jax.ShapeDtypeStruct((width, tokens), BF16),
-            jax.ShapeDtypeStruct((rank, width), F32),
-            jax.ShapeDtypeStruct((rank, cols), F32),
+            vm((cols, tokens), BF16), vm((width, tokens), BF16), vm((rank, width), F32), vm((rank, cols), F32)
         ),
         in_specs=[pl.BlockSpec(memory_space=pltpu.HBM)] * 7,
         out_specs=(inside, anywhere, inside, inside),
         scratch_shapes=scratch,
-        compiler_params=pltpu.CompilerParams(collective_id=0, has_side_effects=True),
+        compiler_params=pltpu.CompilerParams(collective_id=0, has_side_effects=True, vmem_limit_bytes=58 << 20),
         name="adapter_step",
     )(index, table, grad.T, up[0], down[0].T, weight, hidden.T)
     results = (values, hidden_grad, down_t, up_grad)
@@ -490,7 +473,8 @@
         out_shape=tuple(jax.ShapeDtypeStruct(r.shape, r.dtype) for r in results),
         in_specs=[anywhere] * 4,
         out_specs=(pl.BlockSpec(memory_space=pltpu.HBM),) * 4,
-        scratch_shapes=[vm(r.shape, r.dtype) for r in results] + [dma((2, 16))],
+        scratch_shapes=[dma((4,))],
+        compiler_params=pltpu.CompilerParams(vmem_limit_bytes=4 << 20),
         name="place_results",
     )(*results)
     return values.T, hidden_grad.T, down_t.T[None], up_grad[None]

time: 63.7 us -> 62.1 us (0.975)
  Pallas kernels: 62.9 us -> 61.3 us
    pallas_call x1, Pallas kernels: 2.46 us -> 1.19 us  [local(): pl.pallas_call(place_results, out_shape=tuple((jax.ShapeDtypeStruct(r.sha...]
where the time goes in v3:
time: 62.1 us; the launch traced here: 61.9 us
  Pallas kernels  61.3 us (99%)
  between operations  0.64 us (1%)
    pallas_call x1, Pallas kernels, local(): pl.pallas_call(functools.partial(kernel, ny, nl, nz), out_shape=(vm((cols...  60.1 us

profile of v3, /device:TPU:1, one launch (start us, length us, event | category | flops | bytes accessed | tf_op | source)
XLA Modules:
  0.0 61.9 jit_solution(8649853985542394400)
XLA Ops:
  0.6 60.1 %adapter_step.1 = (bf16[64,1536]{1,0:T(8,128)(2,1)S(1)}, bf16[448,1536]{1,0:T(8,128)(2,1)S(1)}, f32[32,448]{1,0:T(8,128)S(1)}, f32[32,64]{1,0:T(8,128)S(1)}) custom-call(s32[2]{0:T(128)} %idx_hbm.1, s32[64]{0:T(128)} %tab_hbm.1, bf16[64,1536]{1,0:T(8,128)(2,1)} %bitcast.13, bf16[32,64]{1,0:T(8,128)(2,1)} %bitcast.15, bf16[32,448]{1,0:T(8,128)(2,1)} %bitcast.14, ...), custom_call_target="tpu_custom_call" | custom-call | tf_op jit(solution)/shard_map/adapter_step/pallas_call | solution.py:459
  60.7 1.2 %place_results.1 = (bf16[64,1536]{1,0:T(8,128)(2,1)}, bf16[448,1536]{1,0:T(8,128)(2,1)}, f32[32,448]{1,0:T(8,128)}, f32[32,64]{1,0:T(8,128)}) custom-call(bf16[64,1536]{1,0:T(8,128)(2,1)S(1)} %get-tuple-element.12.refs_0_, bf16[448,1536]{1,0:T(8,128)(2,1)S(1)} %get-tuple-element.13.refs_1_, f32[32,448]{1,0:T(8,128)S(1)} %get-tuple-element.14.refs_2_, ...), custom_call_target="tpu_custom_call" | custom-call | tf_op jit(solution)/shard_map/place_results/pallas_call | solution.py:471

commit v4 on v3

--- a/solution.py
+++ b/solution.py
@@ -33,6 +33,10 @@
 def split(v):
     hi = v.astype(BF16)
     return hi, (v - hi.astype(F32)).astype(BF16)
+
+
+def far_first(n):
+    return sorted(range(1, n), key=lambda o: -min(o, n - o))
 
 
 def pieces(width):
@@ -116,7 +120,7 @@
                 block(out, 0 if same else o, size), block(into, o, size),
                 send_sem.at[o], recv_sem.at[o], peer(o),
             )
-            for o in range(1, n)
+            for o in far_first(n)
         ]
 
     def arrive(copies):
@@ -223,11 +227,20 @@
     got_lb = exchange(line_b_out, line_b, 2 * rank, lb_s, lb_r, line_peer, nl)
     got_la = [pick_a(0)]
     ag_serve(0, 1)
+    per_tile = 128 // (2 * rank)
+    across = []
+    for i in range(nl // per_tile):
+        q = i * per_tile
+        across.append(jnp.where(low_half, ids[q * 8 + 2 : q * 8 + 3, :], ids[q * 8 + 10 : q * 8 + 11, :]))
+    across = jnp.concatenate(across, axis=1)
+    shape = (ny * rank, nl * 2 * rank)
+    slot_out = (xx * ny + lax.rem(y + lax.shift_right_logical(iota((ny * rank, 1), 0), 5), ny)) * 2 + c
+    m2[...] = onehot((slot_out == across) & ((iota(shape, 1) & 31) == (iota(shape, 0) & 31)))
     arrive(got_lb)
     mine = gathered(line_b_out, line_b, 2 * rank, nl)
     z_b[z] = (mine[0:rank, :] + swapped(mine[rank:, :])).astype(BF16)
     got_zb = [
-        send(z_b.at[z], z_b.at[z], zb_s.at[o], zb_r.at[o], z_peer(o)) for o in range(1, nz)
+        send(z_b.at[z], z_b.at[z], zb_s.at[o], zb_r.at[o], z_peer(o)) for o in far_first(nz)
     ]
     ag_serve(1, 0)
     got_la += [pick_a(p) for p in parts[1:]]
@@ -245,6 +258,10 @@
         low[2 * s * rank : (2 * s + 1) * rank, :] = hi
         low[(2 * s + 1) * rank : (2 * s + 2) * rank, :] = rest
 
+    for p in parts:
+        at, size = cuts[p]
+        turn = onehot(iota((size, size), 0) == iota((size, size), 1))
+        a_rows[at : at + size, :] = nt(turn, ab[p][...]).astype(BF16)
     ag_serve(2, 1)
     arrive(got_zb)
     blocks = [z_b[j].astype(F32) for j in range(nz)]
@@ -269,9 +286,11 @@
 
     def rs_go(direction, h, t):
         n = hops[direction][h]
-        value = contribution(toward(direction, n - t), h)
+        j = toward(direction, n - t)
         if t:
-            value = value + rs_recv[direction, h, t - 1].astype(F32)
+            value = pb[j, h * part_rows : (h + 1) * part_rows, :] + rs_recv[direction, h, t - 1].astype(F32)
+        else:
+            value = contribution(j, h)
         rs_send[direction, h, t] = value.astype(BF16)
         rs[direction, h, t] = send(
             rs_send.at[direction, h, t], rs_recv.at[direction, h, t],
@@ -290,10 +309,13 @@
                     if t + 1 < n:
                         rs_go(direction, h, t + 1)
 
-    for h in range(QUARTERS):
-        for direction in range(2):
-            if hops[direction][h]:
-                rs_go(direction, h, 0)
+    def rs_begin(side):
+        for h in [h for h in range(QUARTERS) if h * 2 // QUARTERS == side]:
+            for direction in range(2):
+                if hops[direction][h]:
+                    rs_go(direction, h, 0)
+
+    rs_begin(0)
 
     for t in range(most):
         ag_serve(t, 0, 1)
@@ -324,22 +346,8 @@
         u_out[2 * i + 1] = jnp.where(low_half, swapped(t0), t1).astype(BF16)
     got_zu = [
         send(u_out.at[lax.rem(z + o, nz)], u_in.at[o], zu_s.at[o], zu_r.at[o], z_peer(o))
-        for o in range(1, nz)
+        for o in far_first(nz)
     ]
-    per_tile = 128 // (2 * rank)
-    across = []
-    for i in range(nl // per_tile):
-        q = i * per_tile
-        across.append(jnp.where(low_half, ids[q * 8 + 2 : q * 8 + 3, :], ids[q * 8 + 10 : q * 8 + 11, :]))
-    across = jnp.concatenate(across, axis=1)
-    shape = (ny * rank, nl * 2 * rank)
-    slot_out = (xx * ny + lax.rem(y + lax.shift_right_logical(iota((ny * rank, 1), 0), 5), ny)) * 2 + c
-    m2[...] = onehot((slot_out == across) & ((iota(shape, 1) & 31) == (iota(shape, 0) & 31)))
-    for p in parts:
-        at, size = cuts[p]
-        turn = onehot(iota((size, size), 0) == iota((size, size), 1))
-        a_rows[at : at + size, :] = nt(turn, ab[p][...]).astype(BF16)
-
     def input_grad(s):
         def body(step, carry):
             here = pl.ds(pl.multiple_of(step * chunk, chunk), chunk)
@@ -356,9 +364,20 @@
         copy.start()
         return copy
 
-    rs_serve(0, 0)
-    stores = [input_grad(0)]
-    rs_serve(0, 1)
+    rs_begin(1)
+
+    for s in range(2):
+        turned = bt[s].reshape(nz * cols, 2 * rank)
+
+        def adapt(step, carry):
+            here = pl.ds(pl.multiple_of(step * chunk, chunk), chunk)
+            at = pl.ds(pl.multiple_of(s * rows + step * chunk, chunk), chunk)
+            part = nn(turned, low[2 * s * rank : 2 * (s + 1) * rank, here])
+            pb[:, :, at] += part.reshape(nz, cols, chunk)
+            return carry
+
+        lax.fori_loop(0, rows // chunk, adapt, 0)
+
     got_cd, own_d = [], []
 
     def spread_d(p):
@@ -370,7 +389,10 @@
         )
         own_d.append(summed[0:rank, :])
 
+    rs_serve(0, 0)
+    stores = [input_grad(0)]
     spread_d(0)
+    rs_serve(0, 1)
     arrive(got_zu)
     total = u_out[z].astype(F32)
     for o in range(1, nz):
@@ -382,17 +404,18 @@
     for p in parts[1:]:
         spread_d(p)
     rs_serve(1, 1)
+    stores.append(input_grad(1))
+    rs_serve(2, 0)
     arrive(got_lu)
     summed_u = nn(m2[...], line_u[...])
     col_u_out[...] = summed_u.astype(BF16)
     got_cu = exchange(col_u_out, col_u, rank, cu_s, cu_r, col_peer, ny)
     own_u = summed_u[0:rank, :]
-    stores.append(input_grad(1))
     for t in range(2, most):
         rs_serve(t, 0)
         rs_serve(t, 1)
     for h in range(QUARTERS):
-        value = contribution(z, h)
+        value = pb[z, h * part_rows : (h + 1) * part_rows, :]
         for direction in range(2):
             n = hops[direction][h]
             if n:

time: 62.1 us -> 60.7 us (0.977)
  Pallas kernels: 61.3 us -> 60 us
    pallas_call x1, Pallas kernels: 60.1 us -> 58.8 us  [local(): pl.pallas_call(functools.partial(kernel, ny, nl, nz), out_shape=(vm((cols...]
where the time goes in v4:
time: 60.7 us; the launch traced here: 60.6 us
  Pallas kernels  60 us (99%)
  between operations  0.64 us (1%)
    pallas_call x1, Pallas kernels, local(): pl.pallas_call(functools.partial(kernel, ny, nl, nz), out_shape=(vm((cols...  58.8 us

profile of v4, /device:TPU:1, one launch (start us, length us, event | category | flops | bytes accessed | tf_op | source)
XLA Modules:
  0.0 60.6 jit_solution(7734865489707552533)
XLA Ops:
  0.6 58.8 %adapter_step.1 = (bf16[64,1536]{1,0:T(8,128)(2,1)S(1)}, bf16[448,1536]{1,0:T(8,128)(2,1)S(1)}, f32[32,448]{1,0:T(8,128)S(1)}, f32[32,64]{1,0:T(8,128)S(1)}) custom-call(s32[2]{0:T(128)} %idx_hbm.1, s32[64]{0:T(128)} %tab_hbm.1, bf16[64,1536]{1,0:T(8,128)(2,1)} %bitcast.13, bf16[32,64]{1,0:T(8,128)(2,1)} %bitcast.15, bf16[32,448]{1,0:T(8,128)(2,1)} %bitcast.14, ...), custom_call_target="tpu_custom_call" | custom-call | tf_op jit(solution)/shard_map/adapter_step/pallas_call | solution.py:482
  59.4 1.2 %place_results.1 = (bf16[64,1536]{1,0:T(8,128)(2,1)}, bf16[448,1536]{1,0:T(8,128)(2,1)}, f32[32,448]{1,0:T(8,128)}, f32[32,64]{1,0:T(8,128)}) custom-call(bf16[64,1536]{1,0:T(8,128)(2,1)S(1)} %get-tuple-element.12.refs_0_, bf16[448,1536]{1,0:T(8,128)(2,1)S(1)} %get-tuple-element.13.refs_1_, f32[32,448]{1,0:T(8,128)S(1)} %get-tuple-element.14.refs_2_, ...), custom_call_target="tpu_custom_call" | custom-call | tf_op jit(solution)/shard_map/place_results/pallas_call | solution.py:494

commit v5 on v4

--- a/solution.py
+++ b/solution.py
@@ -10,6 +10,13 @@
 F32 = jnp.float32
 BF16 = jnp.bfloat16
 MESH = pl.DeviceIdType.MESH
+ORDER = (
+    "base", "pass00", "masks", "pass01", "b1", "a0", "pass10", "a1",
+    "pass11", "b2", "pass20", "masks2", "pass21", "low", "b3", "first",
+    "gather", "down", "up", "second", "adapt", "turn", "ring00", "grad0",
+    "down0", "ring01", "up1", "ring10", "down1", "ring11", "grad1", "ring20",
+    "up2", "ring21", "ring30", "ring31",
+)
 QUARTERS = 4
 NY = 8
 
@@ -188,28 +195,33 @@
         exchange(col_a[p], col_a[p], rank, ca_s.at[p], ca_r.at[p], col_peer, ny, same=True) for p in parts
     ]
 
-    loads[-2].wait()
     square = onehot(iota((features, features), 0) == iota((features, features), 1))
-    wt[...] = nt(square, w[...]).astype(BF16)
-    loads[-1].wait()
-
-    def base(step, carry):
-        at = pl.ds(pl.multiple_of(step * chunk, chunk), chunk)
-        part = nn(wt[...], x[:, at])
-        for j in range(nz):
-            pb[j, :, at] = part[j * cols : (j + 1) * cols, :]
-        return carry
-
-    lax.fori_loop(0, tokens // chunk, base, 0)
-
-    arrive(got_ids)
-    slot_in = (xx * ny + lax.rem(y + ny - lax.shift_right_logical(iota((rank, ny * rank), 1), 5), ny)) * 2 + c
-    same_rank = (iota((rank, ny * rank), 1) & 31) == iota((rank, ny * rank), 0)
-    for p in range(nl):
-        q = (nl - p) % nl
-        for s in range(2):
-            own = ids[q * 8 + s : q * 8 + s + 1, :][:, 0:1]
-            m1[(p * 2 + s) * rank : (p * 2 + s + 1) * rank, :] = onehot((slot_in == own) & same_rank)
+    tiles = features // 128
+    got_lb, got_la, got_zb, up = [], [], [], []
+
+    def base_blocks():
+        loads[-2].wait()
+        wt[...] = nt(square, w[...]).astype(BF16)
+        loads[-1].wait()
+
+        def base(step, carry):
+            at = pl.ds(pl.multiple_of(step * chunk, chunk), chunk)
+            part = nn(wt[...], x[:, at])
+            for j in range(nz):
+                pb[j, :, at] = part[j * cols : (j + 1) * cols, :]
+            return carry
+
+        lax.fori_loop(0, tokens // chunk, base, 0)
+
+    def masks_in():
+        arrive(got_ids)
+        slot_in = (xx * ny + lax.rem(y + ny - lax.shift_right_logical(iota((rank, ny * rank), 1), 5), ny)) * 2 + c
+        same_rank = (iota((rank, ny * rank), 1) & 31) == iota((rank, ny * rank), 0)
+        for p in range(nl):
+            q = (nl - p) % nl
+            for s in range(2):
+                own = ids[q * 8 + s : q * 8 + s + 1, :][:, 0:1]
+                m1[(p * 2 + s) * rank : (p * 2 + s + 1) * rank, :] = onehot((slot_in == own) & same_rank)
     def gathered(out, into, size, n):
         total = out[0:size, :].astype(F32)
         for o in range(1, n):
@@ -219,61 +231,59 @@
     def pick_a(p):
         arrive(got_ca[p])
         line_a_out[p][...] = nn(m1[...], col_a[p][...]).astype(BF16)
-        return exchange(line_a_out[p], line_a[p], 2 * rank, la_s.at[p], la_r.at[p], line_peer, nl)
-
-    ag_serve(0, 0)
-    arrive(got_cb)
-    line_b_out[...] = nn(m1[...], col_b[...]).astype(BF16)
-    got_lb = exchange(line_b_out, line_b, 2 * rank, lb_s, lb_r, line_peer, nl)
-    got_la = [pick_a(0)]
-    ag_serve(0, 1)
-    per_tile = 128 // (2 * rank)
-    across = []
-    for i in range(nl // per_tile):
-        q = i * per_tile
-        across.append(jnp.where(low_half, ids[q * 8 + 2 : q * 8 + 3, :], ids[q * 8 + 10 : q * 8 + 11, :]))
-    across = jnp.concatenate(across, axis=1)
-    shape = (ny * rank, nl * 2 * rank)
-    slot_out = (xx * ny + lax.rem(y + lax.shift_right_logical(iota((ny * rank, 1), 0), 5), ny)) * 2 + c
-    m2[...] = onehot((slot_out == across) & ((iota(shape, 1) & 31) == (iota(shape, 0) & 31)))
-    arrive(got_lb)
-    mine = gathered(line_b_out, line_b, 2 * rank, nl)
-    z_b[z] = (mine[0:rank, :] + swapped(mine[rank:, :])).astype(BF16)
-    got_zb = [
-        send(z_b.at[z], z_b.at[z], zb_s.at[o], zb_r.at[o], z_peer(o)) for o in far_first(nz)
-    ]
-    ag_serve(1, 0)
-    got_la += [pick_a(p) for p in parts[1:]]
-    ag_serve(1, 1)
-    ag_serve(2, 0)
-    for p in parts:
-        arrive(got_la[p])
-        ab[p][...] = gathered(line_a_out[p], line_a[p], 2 * rank, nl).astype(BF16)
-    for s in range(2):
-        part = 0.0
+        got_la.append(exchange(line_a_out[p], line_a[p], 2 * rank, la_s.at[p], la_r.at[p], line_peer, nl))
+
+    def pick_b():
+        arrive(got_cb)
+        line_b_out[...] = nn(m1[...], col_b[...]).astype(BF16)
+        got_lb.extend(exchange(line_b_out, line_b, 2 * rank, lb_s, lb_r, line_peer, nl))
+
+    def masks_out():
+        per_tile = 128 // (2 * rank)
+        across = []
+        for i in range(nl // per_tile):
+            q = i * per_tile
+            across.append(jnp.where(low_half, ids[q * 8 + 2 : q * 8 + 3, :], ids[q * 8 + 10 : q * 8 + 11, :]))
+        across = jnp.concatenate(across, axis=1)
+        shape = (ny * rank, nl * 2 * rank)
+        slot_out = (xx * ny + lax.rem(y + lax.shift_right_logical(iota((ny * rank, 1), 0), 5), ny)) * 2 + c
+        m2[...] = onehot((slot_out == across) & ((iota(shape, 1) & 31) == (iota(shape, 0) & 31)))
+    def share_b():
+        arrive(got_lb)
+        mine = gathered(line_b_out, line_b, 2 * rank, nl)
+        z_b[z] = (mine[0:rank, :] + swapped(mine[rank:, :])).astype(BF16)
+        got_zb[:] = [
+            send(z_b.at[z], z_b.at[z], zb_s.at[o], zb_r.at[o], z_peer(o)) for o in far_first(nz)
+        ]
+    def low_rank():
+        for p in parts:
+            arrive(got_la[p])
+            ab[p][...] = gathered(line_a_out[p], line_a[p], 2 * rank, nl).astype(BF16)
+        for s in range(2):
+            part = 0.0
+            for p in parts:
+                at, size = cuts[p]
+                part = part + nn(ab[p][s * rank : (s + 1) * rank, :], x[at : at + size, s * rows : (s + 1) * rows])
+            hi, rest = split(part)
+            low[2 * s * rank : (2 * s + 1) * rank, :] = hi
+            low[(2 * s + 1) * rank : (2 * s + 2) * rank, :] = rest
+
+    def turn_a():
         for p in parts:
             at, size = cuts[p]
-            part = part + nn(ab[p][s * rank : (s + 1) * rank, :], x[at : at + size, s * rows : (s + 1) * rows])
-        hi, rest = split(part)
-        low[2 * s * rank : (2 * s + 1) * rank, :] = hi
-        low[(2 * s + 1) * rank : (2 * s + 2) * rank, :] = rest
-
-    for p in parts:
-        at, size = cuts[p]
-        turn = onehot(iota((size, size), 0) == iota((size, size), 1))
-        a_rows[at : at + size, :] = nt(turn, ab[p][...]).astype(BF16)
-    ag_serve(2, 1)
-    arrive(got_zb)
-    blocks = [z_b[j].astype(F32) for j in range(nz)]
-    tiles = features // 128
-    up = [
-        [jnp.where(low_half, blocks[2 * i], swapped(blocks[2 * i + 1])) for i in range(tiles)],
-        [jnp.where(low_half, swapped(blocks[2 * i]), blocks[2 * i + 1]) for i in range(tiles)],
-    ]
-    up = [jnp.concatenate(parts, axis=1).astype(BF16) for parts in up]
-    for s in range(2):
-        turned = nt(square, jnp.concatenate([up[s], up[s]], axis=0)).astype(BF16)
-        bt[s] = turned.reshape(nz, cols, 2 * rank)
+            turn = onehot(iota((size, size), 0) == iota((size, size), 1))
+            a_rows[at : at + size, :] = nt(turn, ab[p][...]).astype(BF16)
+    def whole_b():
+        arrive(got_zb)
+        blocks = [z_b[j].astype(F32) for j in range(nz)]
+        both = [
+            [jnp.where(low_half, blocks[2 * i], swapped(blocks[2 * i + 1])) for i in range(tiles)],
+            [jnp.where(low_half, swapped(blocks[2 * i]), blocks[2 * i + 1]) for i in range(tiles)],
+        ]
+        up[:] = [jnp.concatenate(half, axis=1).astype(BF16) for half in both]
+        for s in range(2):
+            turned = nt(square, jnp.concatenate([up[s], up[s]], axis=0)).astype(BF16)
+            bt[s] = turned.reshape(nz, cols, 2 * rank)
 
     def contribution(j, h):
         at = slice(h * part_rows, (h + 1) * part_rows)
@@ -315,39 +325,43 @@
                 if hops[direction][h]:
                     rs_go(direction, h, 0)
 
-    rs_begin(0)
-
-    for t in range(most):
-        ag_serve(t, 0, 1)
-
     def grads(s, at=None):
         at = pl.ds(s * rows, rows) if at is None else at
         return gbuf[:, :, at].reshape(nz * cols, at.size)
 
-    got_ld = []
-    for s in range(2):
-        back_t[s * rank : (s + 1) * rank, :] = nn(up[s], grads(s)).astype(BF16)
-    for p in parts:
-        at, size = cuts[p]
+    got_ld, got_zu, got_cd, own_d, stores, late = [], [], [], [], [], {}
+
+    def gather_end():
+        for t in range(most):
+            ag_serve(t, 0, 1)
+
+    def begin_d():
         for s in range(2):
-            line_d[p][s * rank : (s + 1) * rank, :] = nt(
-                back_t[s * rank : (s + 1) * rank, :], x[at : at + size, s * rows : (s + 1) * rows]
-            ).astype(BF16)
-        got_ld.append(
-            exchange(line_d[p], line_d[p], 2 * rank, ld_s.at[p], ld_r.at[p], line_peer, nl, same=True)
+            back_t[s * rank : (s + 1) * rank, :] = nn(up[s], grads(s)).astype(BF16)
+        for p in parts:
+            at, size = cuts[p]
+            for s in range(2):
+                line_d[p][s * rank : (s + 1) * rank, :] = nt(
+                    back_t[s * rank : (s + 1) * rank, :], x[at : at + size, s * rows : (s + 1) * rows]
+                ).astype(BF16)
+            got_ld.append(
+                exchange(line_d[p], line_d[p], 2 * rank, ld_s.at[p], ld_r.at[p], line_peer, nl, same=True)
+            )
+
+    def begin_u():
+        ups = []
+        for s in range(2):
+            both = nt(low[2 * s * rank : 2 * (s + 1) * rank, :], grads(s))
+            ups.append(both[0:rank, :] + both[rank:, :])
+        for i in range(tiles):
+            t0, t1 = (u[:, i * 128 : (i + 1) * 128] for u in ups)
+            u_out[2 * i] = jnp.where(low_half, t0, swapped(t1)).astype(BF16)
+            u_out[2 * i + 1] = jnp.where(low_half, swapped(t0), t1).astype(BF16)
+        got_zu.extend(
+            send(u_out.at[lax.rem(z + o, nz)], u_in.at[o], zu_s.at[o], zu_r.at[o], z_peer(o))
+            for o in far_first(nz)
         )
-    ups = []
-    for s in range(2):
-        both = nt(low[2 * s * rank : 2 * (s + 1) * rank, :], grads(s))
-        ups.append(both[0:rank, :] + both[rank:, :])
-    for i in range(tiles):
-        t0, t1 = (u[:, i * 128 : (i + 1) * 128] for u in ups)
-        u_out[2 * i] = jnp.where(low_half, t0, swapped(t1)).astype(BF16)
-        u_out[2 * i + 1] = jnp.where(low_half, swapped(t0), t1).astype(BF16)
-    got_zu = [
-        send(u_out.at[lax.rem(z + o, nz)], u_in.at[o], zu_s.at[o], zu_r.at[o], z_peer(o))
-        for o in far_first(nz)
-    ]
+
     def input_grad(s):
         def body(step, carry):
             here = pl.ds(pl.multiple_of(step * chunk, chunk), chunk)
@@ -362,23 +376,20 @@
         at = pl.ds(s * rows, rows)
         copy = pltpu.make_async_copy(hg.at[:, at], hgrad_hbm.at[:, at], out_sem.at[s])
         copy.start()
-        return copy
-
-    rs_begin(1)
-
-    for s in range(2):
-        turned = bt[s].reshape(nz * cols, 2 * rank)
-
-        def adapt(step, carry):
-            here = pl.ds(pl.multiple_of(step * chunk, chunk), chunk)
-            at = pl.ds(pl.multiple_of(s * rows + step * chunk, chunk), chunk)
-            part = nn(turned, low[2 * s * rank : 2 * (s + 1) * rank, here])
-            pb[:, :, at] += part.reshape(nz, cols, chunk)
-            return carry
-
-        lax.fori_loop(0, rows // chunk, adapt, 0)
-
-    got_cd, own_d = [], []
+        stores.append(copy)
+
+    def adapt_all():
+        for s in range(2):
+            turned = bt[s].reshape(nz * cols, 2 * rank)
+
+            def adapt(step, carry):
+                here = pl.ds(pl.multiple_of(step * chunk, chunk), chunk)
+                at = pl.ds(pl.multiple_of(s * rows + step * chunk, chunk), chunk)
+                part = nn(turned, low[2 * s * rank : 2 * (s + 1) * rank, here])
+                pb[:, :, at] += part.reshape(nz, cols, chunk)
+                return carry
+
+            lax.fori_loop(0, rows // chunk, adapt, 0)
 
     def spread_d(p):
         arrive(got_ld[p])
@@ -389,31 +400,41 @@
         )
         own_d.append(summed[0:rank, :])
 
-    rs_serve(0, 0)
-    stores = [input_grad(0)]
-    spread_d(0)
-    rs_serve(0, 1)
-    arrive(got_zu)
-    total = u_out[z].astype(F32)
-    for o in range(1, nz):
-        total = total + u_in[o].astype(F32)
-    for s, part in enumerate((total, swapped(total))):
-        line_u[s * rank : (s + 1) * rank, :] = jnp.where(low_half, part, 0.0).astype(BF16)
-    got_lu = exchange(line_u, line_u, 2 * rank, lu_s, lu_r, line_peer, nl, same=True)
-    rs_serve(1, 0)
-    for p in parts[1:]:
-        spread_d(p)
-    rs_serve(1, 1)
-    stores.append(input_grad(1))
-    rs_serve(2, 0)
-    arrive(got_lu)
-    summed_u = nn(m2[...], line_u[...])
-    col_u_out[...] = summed_u.astype(BF16)
-    got_cu = exchange(col_u_out, col_u, rank, cu_s, cu_r, col_peer, ny)
-    own_u = summed_u[0:rank, :]
-    for t in range(2, most):
-        rs_serve(t, 0)
-        rs_serve(t, 1)
+    def middle_u():
+        arrive(got_zu)
+        total = u_out[z].astype(F32)
+        for o in range(1, nz):
+            total = total + u_in[o].astype(F32)
+        for s, part in enumerate((total, swapped(total))):
+            line_u[s * rank : (s + 1) * rank, :] = jnp.where(low_half, part, 0.0).astype(BF16)
+        late["line"] = exchange(line_u, line_u, 2 * rank, lu_s, lu_r, line_peer, nl, same=True)
+
+    def spread_u():
+        arrive(late["line"])
+        summed = nn(m2[...], line_u[...])
+        col_u_out[...] = summed.astype(BF16)
+        late["column"] = exchange(col_u_out, col_u, rank, cu_s, cu_r, col_peer, ny)
+        late["own"] = summed[0:rank, :]
+
+    fronts = len(cuts) // 2
+    steps = {
+        "base": base_blocks, "masks": masks_in, "masks2": masks_out, "b1": pick_b, "b2": share_b, "b3": whole_b,
+        "a0": lambda: pick_a(0), "a1": lambda: [pick_a(p) for p in parts[1:]], "low": low_rank, "turn": turn_a,
+        "gather": gather_end, "first": lambda: rs_begin(0), "second": lambda: rs_begin(1),
+        "down": begin_d, "up": begin_u, "adapt": adapt_all,
+        "grad0": lambda: input_grad(0), "grad1": lambda: input_grad(1),
+        "down0": lambda: [spread_d(p) for p in parts if p < max(fronts, 1)],
+        "down1": lambda: [spread_d(p) for p in parts if p >= max(fronts, 1)],
+        "up1": middle_u, "up2": spread_u,
+    }
+    for t in range(4):
+        for side in range(2):
+            steps[f"ring{t}{side}"] = functools.partial(rs_serve, t, side)
+            steps[f"pass{t}{side}"] = functools.partial(ag_serve, t, side)
+    for name in ORDER:
+        if name[:4] not in ("ring", "pass") or int(name[4]) < most:
+            steps[name]()
+
     for h in range(QUARTERS):
         value = pb[z, h * part_rows : (h + 1) * part_rows, :]
         for direction in range(2):
@@ -427,7 +448,8 @@
         for o in range(1, ny):
             own_d[p] = own_d[p] + col_d[p][o * rank : (o + 1) * rank, :].astype(F32)
         down_ref[:, cuts[p][0] : cuts[p][0] + cuts[p][1]] = own_d[p]
-    arrive(got_cu)
+    arrive(late["column"])
+    own_u = late["own"]
     for o in range(1, ny):
         own_u = own_u + col_u[o * rank : (o + 1) * rank, :].astype(F32)
     up_ref[...] = own_u[:, 0:cols]

time: 60.7 us -> 58.3 us (0.960)
  Pallas kernels: 60 us -> 57.5 us
    pallas_call x1, Pallas kernels: 58.8 us -> 56.3 us  [local(): pl.pallas_call(functools.partial(kernel, ny, nl, nz), out_shape=(vm((cols...]
where the time goes in v5:
time: 58.3 us; the launch traced here: 58.1 us
  Pallas kernels  57.5 us (99%)
  between operations  0.64 us (1%)
    pallas_call x1, Pallas kernels, local(): pl.pallas_call(functools.partial(kernel, ny, nl, nz), out_shape=(vm((cols...  56.3 us
    pallas_call x1, Pallas kernels, local(): pl.pallas_call(place_results, out_shape=tuple((jax.ShapeDtypeStruct(r.sha...  1.19 us

profile of v5, /device:TPU:1, one launch (start us, length us, event | category | flops | bytes accessed | tf_op | source)
XLA Modules:
  0.0 58.1 jit_solution(11010568428926460557)
XLA Ops:
  0.6 56.3 %adapter_step.1 = (bf16[64,1536]{1,0:T(8,128)(2,1)S(1)}, bf16[448,1536]{1,0:T(8,128)(2,1)S(1)}, f32[32,448]{1,0:T(8,128)S(1)}, f32[32,64]{1,0:T(8,128)S(1)}) custom-call(s32[2]{0:T(128)} %idx_hbm.1, s32[64]{0:T(128)} %tab_hbm.1, bf16[64,1536]{1,0:T(8,128)(2,1)} %bitcast.13, bf16[32,64]{1,0:T(8,128)(2,1)} %bitcast.15, bf16[32,448]{1,0:T(8,128)(2,1)} %bitcast.14, ...), custom_call_target="tpu_custom_call" | custom-call | tf_op jit(solution)/shard_map/adapter_step/pallas_call | solution.py:504
  57.0 1.2 %place_results.1 = (bf16[64,1536]{1,0:T(8,128)(2,1)}, bf16[448,1536]{1,0:T(8,128)(2,1)}, f32[32,448]{1,0:T(8,128)}, f32[32,64]{1,0:T(8,128)}) custom-call(bf16[64,1536]{1,0:T(8,128)(2,1)S(1)} %get-tuple-element.12.refs_0_, bf16[448,1536]{1,0:T(8,128)(2,1)S(1)} %get-tuple-element.13.refs_1_, f32[32,448]{1,0:T(8,128)S(1)} %get-tuple-element.14.refs_2_, ...), custom_call_target="tpu_custom_call" | custom-call | tf_op jit(solution)/shard_map/place_results/pallas_call | solution.py:516
